TPU v7x, 32 devices: a whole 2x2x4 slice. The times are simulated.
32 devices in a mesh: ctx: 4 (over y, x), wsh: 8 (over z, core).
Axes of the slice: x: 2, y: 2, z: 4, core: 2. Of those that a mesh axis runs over, the one named last changes fastest.
Arguments:
- tokens: bfloat16 [8, 2048, 768], P('wsh', 'ctx'), may hold values from -6 to 6
- cluster_order: int32 [8, 2048], P('wsh', 'ctx'), may hold values from 0 to 2047, as said below
- qkv_weight: bfloat16 [768, 2304], P('wsh'), may hold values from -0.21875 to 0.21875
- query_bias: bfloat16 [768], P('wsh'), may hold values from -3 to 3
- value_bias: bfloat16 [768], P('wsh'), may hold values from -1.25 to 1.25
- out_weight: bfloat16 [768, 768], P('wsh'), may hold values from -1.25 to 1.25
- out_bias: bfloat16 [768], P('wsh'), may hold values from -1.75 to 1.75
- first_gain: bfloat16 [768], P('wsh'), may hold values from 0.25 to 1.75
- first_shift: bfloat16 [768], P('wsh'), may hold values from -1.75 to 1.75
- up_weight: bfloat16 [768, 3072], P('wsh'), may hold values from -0.21875 to 0.21875
- up_bias: bfloat16 [3072], P('wsh'), may hold values from -3 to 3
- down_weight: bfloat16 [3072, 768], P('wsh'), may hold values from -0.109375 to 0.109375
- down_bias: bfloat16 [768], P('wsh'), may hold values from -1.75 to 1.75
- second_gain: bfloat16 [768], P('wsh'), may hold values from 0.25 to 1.75
- second_shift: bfloat16 [768], P('wsh'), may hold values from -1.75 to 1.75
- cotangent: bfloat16 [8, 2048, 768], P('wsh', 'ctx'), may hold values from -6 to 6
Outputs:
- layer_out: bfloat16 [8, 2048, 768], P('wsh', 'ctx')
- grad_tokens: float32 [8, 2048, 768], P('wsh', 'ctx')
- grad_qkv_weight: float32 [768, 2304], P('wsh')
- grad_query_bias: float32 [768], P('wsh')
- grad_value_bias: float32 [768], P('wsh')
- grad_out_weight: float32 [768, 768], P('wsh')
- grad_out_bias: float32 [768], P('wsh')
- grad_first_gain: float32 [768], P('wsh')
- grad_first_shift: float32 [768], P('wsh')
- grad_up_weight: float32 [768, 3072], P('wsh')
- grad_up_bias: float32 [3072], P('wsh')
- grad_down_weight: float32 [3072, 768], P('wsh')
- grad_down_bias: float32 [768], P('wsh')
- grad_second_gain: float32 [768], P('wsh')
- grad_second_shift: float32 [768], P('wsh')
Inputs may be any that keep to these rules, and one draw needn't show every extreme that they name: `cluster_order`: each stream's row is a permutation of its positions. The stream is cut into four documents, each a multiple of 128 tokens long, the longest exactly 1024; the permutation maps every document's positions onto themselves, so each cluster lies within one document.
All inputs are finite; a program needn't handle non-finite values.
Results may differ from a plain program's by a relative error of at most 0.02.
Values may be sent and summed in bfloat16 or wider, within the bound.
A program may use at most 128 MiB of HBM per device.

v0:
```python
import jax
import jax.numpy as jnp
from jax import lax
from jax.sharding import PartitionSpec as P

HEAD_DIM = 64
CLUSTER = 128


epsilon = 1e-05


def inner(left, right):
    return lax.dot_general(
        left, right, (((0,), (0,)), ((), ())), preferred_element_type=jnp.float32
    )


def times_transposed(left, right):
    return lax.dot_general(
        left, right, (((1,), (1,)), ((), ())), preferred_element_type=jnp.float32
    )


def normalize(values):
    centre = values - jnp.mean(values, axis=1, keepdims=True)
    factor = lax.rsqrt(jnp.mean(centre * centre, axis=1, keepdims=True) + epsilon)
    return (centre * factor, factor)


def norm_back(grad_out, normed, factor, gain):
    grad_normed = grad_out * gain
    return factor * (
        grad_normed
        - jnp.mean(grad_normed, axis=1, keepdims=True)
        - normed * jnp.mean(grad_normed * normed, axis=1, keepdims=True)
    )


def on_device(
    tokens,
    cluster_order,
    qkv_weight,
    query_bias,
    value_bias,
    out_weight,
    out_bias,
    first_gain,
    first_shift,
    up_weight,
    up_bias,
    down_weight,
    down_bias,
    second_gain,
    second_shift,
    cotangent,
):
    inputs = tokens[0]
    order = cluster_order[0]
    rows = inputs.shape[0]
    width = inputs.shape[1]
    heads = width // HEAD_DIM
    blocks = rows // CLUSTER
    group_rows = rows * lax.axis_size("ctx")
    factor_qk = HEAD_DIM ** (-0.5)
    (
        whole_qkv,
        whole_qbias,
        whole_vbias,
        whole_out,
        whole_obias,
        whole_gain1,
        whole_shift1,
        whole_up,
        whole_ubias,
        whole_down,
        whole_dbias,
        whole_gain2,
        whole_shift2,
    ) = (
        lax.all_gather(qkv_weight, "wsh", axis=0, tiled=True),
        lax.all_gather(query_bias, "wsh", axis=0, tiled=True),
        lax.all_gather(value_bias, "wsh", axis=0, tiled=True),
        lax.all_gather(out_weight, "wsh", axis=0, tiled=True),
        lax.all_gather(out_bias, "wsh", axis=0, tiled=True),
        lax.all_gather(first_gain, "wsh", axis=0, tiled=True),
        lax.all_gather(first_shift, "wsh", axis=0, tiled=True),
        lax.all_gather(up_weight, "wsh", axis=0, tiled=True),
        lax.all_gather(up_bias, "wsh", axis=0, tiled=True),
        lax.all_gather(down_weight, "wsh", axis=0, tiled=True),
        lax.all_gather(down_bias, "wsh", axis=0, tiled=True),
        lax.all_gather(second_gain, "wsh", axis=0, tiled=True),
        lax.all_gather(second_shift, "wsh", axis=0, tiled=True),
    )
    qkv_shift = jnp.concatenate(
        [
            whole_qbias.astype(jnp.float32),
            jnp.zeros((width,), jnp.float32),
            whole_vbias.astype(jnp.float32),
        ]
    )
    out_shift = whole_obias.astype(jnp.float32)
    gain_one = whole_gain1.astype(jnp.float32)
    shift_one = whole_shift1.astype(jnp.float32)
    up_shift = whole_ubias.astype(jnp.float32)
    down_shift = whole_dbias.astype(jnp.float32)
    gain_two = whole_gain2.astype(jnp.float32)
    shift_two = whole_shift2.astype(jnp.float32)
    own_qkv = (jnp.dot(inputs, whole_qkv, preferred_element_type=jnp.float32) + qkv_shift).astype(
        jnp.bfloat16
    )
    group_qkv = lax.all_gather(own_qkv, "ctx", axis=0, tiled=True)
    picked = jnp.take(group_qkv, order, axis=0)
    query = picked[:, :width].reshape(blocks, CLUSTER, heads, HEAD_DIM)
    keyed = picked[:, width : 2 * width].reshape(blocks, CLUSTER, heads, HEAD_DIM)
    valued = picked[:, 2 * width :].reshape(blocks, CLUSTER, heads, HEAD_DIM)
    places = order.reshape(blocks, CLUSTER)
    visible = (places[:, None, :] <= places[:, :, None])[:, None, :, :]
    scores = (
        jnp.einsum("cihd,cjhd->chij", query, keyed, preferred_element_type=jnp.float32) * factor_qk
    )
    masked = jnp.where(visible, scores, -1e30)
    row_max = jnp.max(masked, axis=3, keepdims=True)
    expd = jnp.where(visible, jnp.exp(masked - row_max), 0.0)
    total = jnp.sum(expd, axis=3, keepdims=True)
    log_total = row_max + jnp.log(total)
    probs = (expd / total).astype(jnp.bfloat16)
    context = (
        jnp.einsum("chij,cjhd->cihd", probs, valued, preferred_element_type=jnp.float32)
        .astype(jnp.bfloat16)
        .reshape(rows, width)
    )
    branch = (jnp.dot(context, whole_out, preferred_element_type=jnp.float32) + out_shift).astype(
        jnp.bfloat16
    )
    spread = jnp.zeros((group_rows, width), jnp.bfloat16).at[order].set(branch)
    attended = lax.psum_scatter(spread, "ctx", scatter_dimension=0, tiled=True).astype(jnp.float32)
    resid = inputs.astype(jnp.float32) + attended
    first_norm, first_factor = normalize(resid)
    first_out = first_norm * gain_one + shift_one
    first_low = first_out.astype(jnp.bfloat16)
    pre_act = jnp.dot(first_low, whole_up, preferred_element_type=jnp.float32) + up_shift
    hidden = jax.nn.gelu(pre_act, approximate=False).astype(jnp.bfloat16)
    second_in = (
        first_out + jnp.dot(hidden, whole_down, preferred_element_type=jnp.float32) + down_shift
    )
    second_norm, second_factor = normalize(second_in)
    layer_out = (second_norm * gain_two + shift_two).astype(jnp.bfloat16)
    grad_top = cotangent[0].astype(jnp.float32)
    grad_gain_two = jnp.sum(grad_top * second_norm, axis=0)
    grad_shift_two = jnp.sum(grad_top, axis=0)
    grad_second = norm_back(grad_top, second_norm, second_factor, gain_two)
    grad_branch2 = grad_second.astype(jnp.bfloat16)
    grad_down_w = inner(hidden, grad_branch2)
    grad_down_b = jnp.sum(grad_branch2.astype(jnp.float32), axis=0)
    grad_hidden = times_transposed(grad_branch2, whole_down)
    slope = (
        0.5 * (1.0 + lax.erf(pre_act * 0.7071067811865476))
        + pre_act * jnp.exp(-0.5 * pre_act * pre_act) * 0.3989422804014327
    )
    grad_pre = (grad_hidden * slope).astype(jnp.bfloat16)
    grad_up_w = inner(first_low, grad_pre)
    grad_up_b = jnp.sum(grad_pre.astype(jnp.float32), axis=0)
    grad_first = grad_second + times_transposed(grad_pre, whole_up)
    grad_gain_one = jnp.sum(grad_first * first_norm, axis=0)
    grad_shift_one = jnp.sum(grad_first, axis=0)
    grad_resid = norm_back(grad_first, first_norm, first_factor, gain_one)
    grad_attended = grad_resid.astype(jnp.bfloat16)
    grad_out_b = jnp.sum(grad_attended.astype(jnp.float32), axis=0)
    group_grads = lax.all_gather(grad_attended, "ctx", axis=0, tiled=True)
    picked_grad = jnp.take(group_grads, order, axis=0)
    grad_out_w = inner(context, picked_grad)
    grad_context = (
        times_transposed(picked_grad, whole_out)
        .astype(jnp.bfloat16)
        .reshape(blocks, CLUSTER, heads, HEAD_DIM)
    )
    again = (
        jnp.einsum("cihd,cjhd->chij", query, keyed, preferred_element_type=jnp.float32) * factor_qk
    )
    probs_full = jnp.where(visible, jnp.exp(jnp.where(visible, again, -1e30) - log_total), 0.0)
    probs_low = probs_full.astype(jnp.bfloat16)
    grad_probs = jnp.einsum(
        "cihd,cjhd->chij", grad_context, valued, preferred_element_type=jnp.float32
    )
    grad_valued = jnp.einsum(
        "chij,cihd->cjhd", probs_low, grad_context, preferred_element_type=jnp.float32
    ).astype(jnp.bfloat16)
    inner_sum = jnp.sum(probs_full * grad_probs, axis=3, keepdims=True)
    grad_scores = (probs_full * (grad_probs - inner_sum)).astype(jnp.bfloat16)
    grad_query = (
        jnp.einsum("chij,cjhd->cihd", grad_scores, keyed, preferred_element_type=jnp.float32)
        * factor_qk
    ).astype(jnp.bfloat16)
    grad_keyed = (
        jnp.einsum("chij,cihd->cjhd", grad_scores, query, preferred_element_type=jnp.float32)
        * factor_qk
    ).astype(jnp.bfloat16)
    grad_picked = jnp.concatenate(
        [
            grad_query.reshape(rows, width),
            grad_keyed.reshape(rows, width),
            grad_valued.reshape(rows, width),
        ],
        axis=1,
    )
    grad_query_b = jnp.sum(grad_picked[:, :width].astype(jnp.float32), axis=0)
    grad_value_b = jnp.sum(grad_picked[:, 2 * width :].astype(jnp.float32), axis=0)
    spread_grad = jnp.zeros((group_rows, 3 * width), jnp.bfloat16).at[order].set(grad_picked)
    own_grad = (
        lax.psum_scatter(spread_grad, "ctx", scatter_dimension=0, tiled=True)
        .astype(jnp.float32)
        .astype(jnp.bfloat16)
    )
    grad_qkv_w = inner(inputs, own_grad)
    grad_inputs = grad_resid + times_transposed(own_grad, whole_qkv)
    totals = (
        lax.psum_scatter(
            grad_qkv_w.astype(jnp.bfloat16), "wsh", scatter_dimension=0, tiled=True
        ).astype(jnp.float32),
        lax.psum_scatter(
            grad_query_b.astype(jnp.bfloat16), "wsh", scatter_dimension=0, tiled=True
        ).astype(jnp.float32),
        lax.psum_scatter(
            grad_value_b.astype(jnp.bfloat16), "wsh", scatter_dimension=0, tiled=True
        ).astype(jnp.float32),
        lax.psum_scatter(
            grad_out_w.astype(jnp.bfloat16), "wsh", scatter_dimension=0, tiled=True
        ).astype(jnp.float32),
        lax.psum_scatter(
            grad_out_b.astype(jnp.bfloat16), "wsh", scatter_dimension=0, tiled=True
        ).astype(jnp.float32),
        lax.psum_scatter(
            grad_gain_one.astype(jnp.bfloat16), "wsh", scatter_dimension=0, tiled=True
        ).astype(jnp.float32),
        lax.psum_scatter(
            grad_shift_one.astype(jnp.bfloat16), "wsh", scatter_dimension=0, tiled=True
        ).astype(jnp.float32),
        lax.psum_scatter(
            grad_up_w.astype(jnp.bfloat16), "wsh", scatter_dimension=0, tiled=True
        ).astype(jnp.float32),
        lax.psum_scatter(
            grad_up_b.astype(jnp.bfloat16), "wsh", scatter_dimension=0, tiled=True
        ).astype(jnp.float32),
        lax.psum_scatter(
            grad_down_w.astype(jnp.bfloat16), "wsh", scatter_dimension=0, tiled=True
        ).astype(jnp.float32),
        lax.psum_scatter(
            grad_down_b.astype(jnp.bfloat16), "wsh", scatter_dimension=0, tiled=True
        ).astype(jnp.float32),
        lax.psum_scatter(
            grad_gain_two.astype(jnp.bfloat16), "wsh", scatter_dimension=0, tiled=True
        ).astype(jnp.float32),
        lax.psum_scatter(
            grad_shift_two.astype(jnp.bfloat16), "wsh", scatter_dimension=0, tiled=True
        ).astype(jnp.float32),
    )
    (
        sum_qkv,
        sum_qbias,
        sum_vbias,
        sum_out,
        sum_obias,
        sum_gain1,
        sum_shift1,
        sum_up,
        sum_ubias,
        sum_down,
        sum_dbias,
        sum_gain2,
        sum_shift2,
    ) = (
        lax.psum(totals[0].astype(jnp.bfloat16), "ctx").astype(jnp.float32),
        lax.psum(totals[1].astype(jnp.bfloat16), "ctx").astype(jnp.float32),
        lax.psum(totals[2].astype(jnp.bfloat16), "ctx").astype(jnp.float32),
        lax.psum(totals[3].astype(jnp.bfloat16), "ctx").astype(jnp.float32),
        lax.psum(totals[4].astype(jnp.bfloat16), "ctx").astype(jnp.float32),
        lax.psum(totals[5].astype(jnp.bfloat16), "ctx").astype(jnp.float32),
        lax.psum(totals[6].astype(jnp.bfloat16), "ctx").astype(jnp.float32),
        lax.psum(totals[7].astype(jnp.bfloat16), "ctx").astype(jnp.float32),
        lax.psum(totals[8].astype(jnp.bfloat16), "ctx").astype(jnp.float32),
        lax.psum(totals[9].astype(jnp.bfloat16), "ctx").astype(jnp.float32),
        lax.psum(totals[10].astype(jnp.bfloat16), "ctx").astype(jnp.float32),
        lax.psum(totals[11].astype(jnp.bfloat16), "ctx").astype(jnp.float32),
        lax.psum(totals[12].astype(jnp.bfloat16), "ctx").astype(jnp.float32),
    )
    return (
        layer_out[None],
        grad_inputs[None],
        sum_qkv,
        sum_qbias,
        sum_vbias,
        sum_out,
        sum_obias,
        sum_gain1,
        sum_shift1,
        sum_up,
        sum_ubias,
        sum_down,
        sum_dbias,
        sum_gain2,
        sum_shift2,
    )


def solution(mesh):
    in_specs = (
        P("wsh", "ctx", None),
        P("wsh", "ctx"),
        P("wsh", None),
        P("wsh"),
        P("wsh"),
        P("wsh", None),
        P("wsh"),
        P("wsh"),
        P("wsh"),
        P("wsh", None),
        P("wsh"),
        P("wsh", None),
        P("wsh"),
        P("wsh"),
        P("wsh"),
        P("wsh", "ctx", None),
    )
    out_specs = (
        P("wsh", "ctx", None),
        P("wsh", "ctx", None),
        P("wsh", None),
        P("wsh"),
        P("wsh"),
        P("wsh", None),
        P("wsh"),
        P("wsh"),
        P("wsh"),
        P("wsh", None),
        P("wsh"),
        P("wsh", None),
        P("wsh"),
        P("wsh"),
        P("wsh"),
    )
    return jax.shard_map(
        on_device, mesh=mesh, in_specs=in_specs, out_specs=out_specs, check_vma=False
    )
```

profile of v0, /device:TPU:0, one launch (start us, length us, event | category | flops | bytes accessed | tf_op | source)
XLA Modules:
  0.0 820.0 jit_solution(3565493798486074965)
XLA Ops:
  8.0 1.3 fusion.86
  10.0 0.8 dynamic-update-slice.1
  11.6 0.8 dynamic-update-slice.4
  12.5 0.8 dynamic-update-slice.3
  13.3 0.8 dynamic-update-slice.2
  15.8 31.6 %all-reduce.18 = (bf16[768]{0:T(1024)(128)(2,1)S(1)}, bf16[768]{0:T(1024)(128)(2,1)S(1)}, bf16[768]{0:T(1024)(128)(2,1)S(1)}, bf16[768]{0:T(1024)(128)(2,1)S(1)}...) all-reduce(bf16[768]{0:T(1024)(128)(2,1)S(1)} %dynamic-update-slice, ...), channel_id=1, replica_groups=mesh['ctx'=4,'wsh'=8] {'wsh'}, use_global_device_ids=true, to_apply=%add.1 | all-reduce | flops 5376 | bytes 21504
  47.5 7.0 all-gather.8.cloned.1.call-done
  54.4 5.6 fusion.18
  61.1 94.4 %all-gather.10.cloned.1.call-done = bf16[2048,2304]{1,0:T(8,128)(2,1)} async-done(((bf16[512,2304]{1,0:T(8,128)(2,1)}), bf16[2048,2304]{1,0:T(8,128)(2,1)}) %all-gather.10.cloned.1.call-update) | async-done | bytes 9437200 | tf_op jit(solution)/shard_map/all_gather | solution.py:112
  155.5 10.8 %gather_fusion = bf16[512,2304]{1,0:T(8,128)(2,1)} fusion(bf16[2048,2304]{1,0:T(8,128)(2,1)} %all-gather.10.cloned.1.call-done, s32[1024]{0:T(1024)S(1)} %pad_clamp_fusion), kind=kCustom, calls=%fused_computation | custom fusion | bytes 4720640 | tf_op jit(solution)/shard_map/jit(_take)/gather | solution.py:113
  166.3 1.9 broadcast_select_fusion
  168.7 1.1 reshape.156
  170.1 1.1 reshape.155
  173.1 0.9 fusion.20
  174.1 1.0 fusion.43
  175.8 4.1 all-gather.12.cloned.1.call-done
  179.8 2.1 add_convert_fusion.1
  182.0 4.7 scatter_custom_fusion
  187.9 13.1 %all-gather = bf16[8,1,384]{2,1,0:T(2,128)(2,1)S(1)} all-gather(bf16[1,1,384]{2,1,0:T(2,128)(2,1)S(1)} %reshape.219), channel_id=1, replica_groups=mesh['ctx'=4,'wsh'=8] {'wsh'}, dimensions={0}, use_global_device_ids=true | all-gather | bytes 6912 | tf_op jit(solution)/shard_map/all_gather | solution.py:89
  201.1 29.5 %reduce-scatter.9.cloned.1.call-done = bf16[512,768]{1,0:T(8,128)(2,1)} async-done(((bf16[2048,768]{1,0:T(8,128)(2,1)}), bf16[512,768]{1,0:T(8,128)(2,1)}) %reduce-scatter.9.cloned.1.call-update) | async-done | bytes 786448 | tf_op jit(solution)/shard_map/reduce_scatter | solution.py:137
  230.6 1.5 fusion.36
  232.1 1.5 multiply_reduce_fusion.4
  233.6 50.2 %all-gather.14.cloned.1.call-done = bf16[768,3072]{1,0:T(8,128)(2,1)} async-done(((bf16[96,3072]{1,0:T(8,128)(2,1)}), bf16[768,3072]{1,0:T(8,128)(2,1)}) %all-gather.14.cloned.1.call-update) | async-done | bytes 4718608 | tf_op jit(solution)/shard_map/all_gather | solution.py:88
  283.8 19.3 %fusion.2 = (bf16[512,3072]{1,0:T(8,128)(2,1)}, f32[512,3072]{1,0:T(8,128)}) fusion(f32[3072]{0:T(1024)S(1)} %bitcast.121, bf16[768,3072]{1,0:T(8,128)(2,1)} %all-gather.14.cloned.1.call-done, f32[768]{0:T(1024)S(1)} %convert_element_type.212, f32[768]{0:T(1024)S(1)} %convert_element_type.211, f32[512]{0:T(512)S(1)} %add_rsqrt_fusion.1, ...), kind=kOutput, calls=%fused_computation.8 | convolution fusion | flops 2522873856 | bytes 15751168 | tf_op jit(solution)/shard_map/dot_general | solution.py:142
  303.1 32.7 %all-gather.16.cloned.1.call-done = bf16[3072,768]{1,0:T(8,128)(2,1)} async-done(((bf16[384,768]{1,0:T(8,128)(2,1)}), bf16[3072,768]{1,0:T(8,128)(2,1)}) %all-gather.16.cloned.1.call-update) | async-done | bytes 4718608 | tf_op jit(solution)/shard_map/all_gather | solution.py:90
  335.8 6.3 fusion.87
  343.8 1.0 copy-done.17
  344.8 4.7 fusion.90
  349.6 3.2 multiply_reduce_fusion.1
  352.9 1.1 copy-done.9
  354.0 1.5 fusion.83
  355.6 42.9 %all-gather.18.cloned.1.call-done = bf16[2048,768]{1,0:T(8,128)(2,1)} async-done(((bf16[512,768]{1,0:T(8,128)(2,1)}), bf16[2048,768]{1,0:T(8,128)(2,1)}) %all-gather.18.cloned.1.call-update) | async-done | bytes 3145744 | tf_op jit(solution)/shard_map/all_gather | solution.py:170
  398.5 5.5 gather_fusion.1
  404.0 3.2 convolution_convert_fusion.4
  407.2 2.3 copy.89
  409.5 2.4 reshape.158
  412.0 3.8 multiply_reduce_fusion
  415.8 1.3 fusion.89
  417.1 1.2 multiply_convert_fusion
  419.5 1.2 fusion.48
  422.9 1.7 pad_maximum_fusion
  424.6 4.3 copy.101
  428.9 10.7 %scatter_custom_fusion.1 = bf16[2048,2304]{1,0:T(8,128)(2,1)} fusion(s32[512]{0:T(512)S(1)} %bitcast.125, bf16[512,2304]{1,0:T(8,128)(2,1)} %copy.101, bf16[]{:T(256)} %constant.42.clone.1), kind=kCustom, calls=%fused_computation.34 | custom fusion | bytes 9437696 | tf_op jit(solution)/shard_map/scatter | solution.py:209
  439.7 95.1 %reduce-scatter.11.cloned.1.call-done = bf16[512,2304]{1,0:T(8,128)(2,1)} async-done(((bf16[2048,2304]{1,0:T(8,128)(2,1)}), bf16[512,2304]{1,0:T(8,128)(2,1)}) %reduce-scatter.11.cloned.1.call-update) | async-done | bytes 2359312 | tf_op jit(solution)/shard_map/reduce_scatter | solution.py:211
  534.8 5.5 fusion.19
  540.3 5.8 copy.107
  546.2 3.3 convolution_convert_fusion.3
  549.5 6.5 convolution_convert_fusion.1
  556.3 7.2 convolution_convert_fusion
  563.6 26.5 %reduce-scatter.19.cloned.1.call-done = bf16[96,2304]{1,0:T(8,128)(2,1)} async-done(((bf16[768,2304]{1,0:T(8,128)(2,1)}), bf16[96,2304]{1,0:T(8,128)(2,1)}) %reduce-scatter.19.cloned.1.call-update) | async-done | bytes 442384
  590.1 2.1 copy.108
  592.2 32.1 %reduce-scatter.13.cloned.1.call-done = bf16[96,768]{1,0:T(8,128)(2,1)} async-done(((bf16[768,768]{1,0:T(8,128)(2,1)}), bf16[96,768]{1,0:T(8,128)(2,1)}) %reduce-scatter.13.cloned.1.call-update) | async-done | bytes 147472 | tf_op jit(solution)/shard_map/reduce_scatter | solution.py:227
  624.3 55.5 %reduce-scatter.15.cloned.1.call-done = bf16[96,3072]{1,0:T(8,128)(2,1)} async-done(((bf16[768,3072]{1,0:T(8,128)(2,1)}), bf16[96,3072]{1,0:T(8,128)(2,1)}) %reduce-scatter.15.cloned.1.call-update) | async-done | bytes 589840 | tf_op jit(solution)/shard_map/reduce_scatter | solution.py:239
  679.8 55.6 %reduce-scatter.17.cloned.1.call-done = bf16[384,768]{1,0:T(8,128)(2,1)} async-done(((bf16[3072,768]{1,0:T(8,128)(2,1)}), bf16[384,768]{1,0:T(8,128)(2,1)}) %reduce-scatter.17.cloned.1.call-update) | async-done | bytes 589840 | tf_op jit(solution)/shard_map/reduce_scatter | solution.py:245
  735.4 1.3 reduce_sum.213
  738.4 26.0 %all-reduce.17 = (bf16[768]{0:T(1024)(128)(2,1)S(1)}, bf16[768]{0:T(1024)(128)(2,1)S(1)}, bf16[768]{0:T(1024)(128)(2,1)S(1)}, bf16[768]{0:T(1024)(128)(2,1)S(1)}...) all-reduce(bf16[768]{0:T(1024)(128)(2,1)S(1)} %dynamic-update-slice, ...), channel_id=1, replica_groups=mesh['ctx'=4,'wsh'=8] {'wsh'}, use_global_device_ids=true, to_apply=%add.7 | all-reduce | flops 9984 | bytes 39936
  765.1 10.0 %all-reduce.19 = (bf16[96]{0:T(256)(128)(2,1)S(1)}, bf16[96]{0:T(256)(128)(2,1)S(1)}, bf16[96]{0:T(256)(128)(2,1)S(1)}, bf16[96]{0:T(256)(128)(2,1)S(1)}, bf16[9...) all-reduce(bf16[96]{0:T(256)(128)(2,1)S(1)} %dynamic-slice.9, ...), channel_id=1, replica_groups=mesh['ctx'=4,'wsh'=8] {'ctx'}, use_global_device_ids=true, to_apply=%region_19.20 | all-reduce | flops 1152 | bytes 4608 | tf_op jit(solution)/shard_map/psum | solution.py:274
  779.7 1.2 fusion.49
  780.9 6.4 add_bitcast_fusion
  787.3 18.7 %all-reduce.23.cloned.1.call-done = (bf16[96,2304]{0,1:T(8,128)(2,1)}, bf16[96,768]{1,0:T(8,128)(2,1)}, bf16[96,3072]{1,0:T(8,128)(2,1)}, bf16[384,768]{1,0:T(8,128)(2,1)}) async-done(((bf16[96,2304]{0,1:T(8,128)(2,1)}, bf16[96,768]{1,0:T(8,128)(2,1)}, bf16[96,3072]{1,0:T(8,128)(2,1)}, bf16[384,768]{1,0:T(8,128)(2,1)}), (bf16[96,2304]{0,1:T(8,128)(2,1)}, bf16[96,768]{1,0:T(8,128)(2,1)}, ...) | async-done | bytes 1769488 | tf_op jit(solution)/shard_map/psum | solution.py:273
  806.0 2.3 copy.102
  808.3 1.6 convert_element_type.240
  809.9 2.2 convert_element_type.247
  812.1 1.1 convert_element_type.250
  (144 shorter events, 20.2 us)
Async XLA Ops:
  7.2 47.3 %all-gather.8.cloned.1.call-start = ((), (), s32[]{:S(2)}) async-start(), calls=%async_computation.6 | async-start | bytes 3981312 | tf_op jit(solution)/shard_map/all_gather | solution.py:81
  7.9 147.6 %all-gather.10.cloned.1.call-start = ((), (), s32[]{:S(2)}) async-start(), calls=%async_computation.7 | async-start | bytes 11796480 | tf_op jit(solution)/shard_map/all_gather | solution.py:112
  47.5 13.4 %copy-start.15 = (s32[1,512]{1,0:T(1,128)S(1)}, s32[1,512]{1,0:T(1,128)}, u32[]{:S(2)}) copy-start(s32[1,512]{1,0:T(1,128)} %param.17) | copy-start | bytes 6148
  60.1 119.7 %all-gather.12.cloned.1.call-start = ((), (), s32[]{:S(2)}) async-start(), calls=%async_computation.8 | async-start | bytes 1327104 | tf_op jit(solution)/shard_map/all_gather | solution.py:84
  60.8 169.7 %reduce-scatter.9.cloned.1.call-start = ((), (), s32[]{:S(2)}) async-start(), calls=%async_computation.9 | async-start | bytes 3932160 | tf_op jit(solution)/shard_map/reduce_scatter | solution.py:137
  169.8 1.8 copy-start.5
  171.1 1.1 copy-start.7
  172.3 1.8 copy-start.12
  173.1 2.0 copy-start
  175.7 6.2 copy-start.11
  181.9 5.9 copy-start.16
  181.9 48.6 %copy-start.2 = (bf16[1,512,768]{2,1,0:T(8,128)(2,1)S(1)}, bf16[1,512,768]{2,1,0:T(8,128)(2,1)}, u32[]{:S(2)}) copy-start(bf16[1,512,768]{2,1,0:T(8,128)(2,1)} %param.16) | copy-start | bytes 2359300
  186.7 97.1 %all-gather.14.cloned.1.call-start = ((), (), s32[]{:S(2)}) async-start(), calls=%async_computation.10 | async-start | bytes 5308416 | tf_op jit(solution)/shard_map/all_gather | solution.py:88
  187.2 148.6 %all-gather.16.cloned.1.call-start = ((), (), s32[]{:S(2)}) async-start(), calls=%async_computation.11 | async-start | bytes 5308416 | tf_op jit(solution)/shard_map/all_gather | solution.py:90
  187.8 210.6 %all-gather.18.cloned.1.call-start = ((), (), s32[]{:S(2)}) async-start(), calls=%async_computation.12 | async-start | bytes 3932160 | tf_op jit(solution)/shard_map/all_gather | solution.py:170
  230.6 53.2 %copy-start.3 = (bf16[512,768]{1,0:T(8,128)(2,1)S(1)}, bf16[512,768]{1,0:T(8,128)(2,1)}, u32[]{:S(2)}) copy-start(bf16[512,768]{1,0:T(8,128)(2,1)} %reduce-scatter.9.cloned.1.call-done) | copy-start | bytes 2359300
  335.8 6.6 copy-start.4
  335.8 8.0 copy-start.20
  342.4 2.4 copy-start.17
  343.2 6.4 slice-start
  343.8 5.8 copy-start.10
  344.8 4.8 slice-start.1
  349.6 3.3 copy-start.19
  352.8 1.1 copy-start.9
  355.5 179.3 %reduce-scatter.11.cloned.1.call-start = ((), (), s32[]{:S(2)}) async-start(), calls=%async_computation.13 | async-start | bytes 11796480 | tf_op jit(solution)/shard_map/reduce_scatter | solution.py:211
  411.9 3.8 copy-start.1
  411.9 3.8 copy-start.13
  417.1 1.2 copy-start.6
  418.3 1.1 copy-start.8
  439.6 150.5 %reduce-scatter.19.cloned.1.call-start = ((), (), s32[]{:S(2)}) async-start(), calls=%async_computation.17 | async-start | bytes 3981312
  546.1 78.2 %reduce-scatter.13.cloned.1.call-start = ((), (), s32[]{:S(2)}) async-start(), calls=%async_computation.14 | async-start | bytes 1327104 | tf_op jit(solution)/shard_map/reduce_scatter | solution.py:227
  549.5 130.3 %reduce-scatter.15.cloned.1.call-start = ((), (), s32[]{:S(2)}) async-start(), calls=%async_computation.15 | async-start | bytes 5308416 | tf_op jit(solution)/shard_map/reduce_scatter | solution.py:239
  556.0 179.4 %reduce-scatter.17.cloned.1.call-start = ((), (), s32[]{:S(2)}) async-start(), calls=%async_computation.16 | async-start | bytes 5308416 | tf_op jit(solution)/shard_map/reduce_scatter | solution.py:245
  563.5 174.5 %copy-start.18 = (bf16[96]{0:T(256)(128)(2,1)S(1)}, bf16[96]{0:T(256)(128)(2,1)}, u32[]{:S(2)}) copy-start(bf16[96]{0:T(256)(128)(2,1)} %param.30) | copy-start | bytes 580
  563.5 242.5 %all-reduce.23.cloned.1.call-start = ((), (), s32[]{:S(2)}) async-start(), calls=%async_computation.18 | async-start | bytes 3833856 | tf_op jit(solution)/shard_map/psum | solution.py:273
  806.0 6.1 copy-start.14
Sparse Core Ops, SparseCore 0:
  9.7 44.7 all-gather.7
  60.2 95.2 all-gather.9
  157.1 22.6 all-gather.11
  186.8 43.7 reduce-scatter.8
  232.0 51.6 all-gather.13
  285.2 50.5 all-gather.15
  355.7 42.7 all-gather.17
  439.8 95.0 reduce-scatter.10
  546.2 43.8 reduce-scatter.18
  592.9 31.3 reduce-scatter.12
  626.7 53.0 reduce-scatter.14
  682.1 53.2 reduce-scatter.16
  739.9 66.1 all-reduce.22
where the time goes:
time: 825 us; the launch traced here: 820 us
  waiting for transfers between devices  547 us (66%)
  matrix products  82 us (10%)
  blocking collectives  80.7 us (10%)
  local copies, waits for them, and re-layouts  68.7 us (8%)
  other arithmetic  24.3 us (3%)
  between operations  16.7 us (2%)
    reduce_scatter x1, waiting for transfers between devices, on_device(): lax.psum_scatter(spread_grad, 'ctx', scatter_dimension=0, tiled=True)  95.1 us
    all_gather x1, waiting for transfers between devices, on_device(): group_qkv = lax.all_gather(own_qkv, 'ctx', axis=0, tiled=True)  94.4 us
    unnamed x2, blocking collectives  57.6 us
    reduce_scatter x1, waiting for transfers between devices, on_device(): lax.psum_scatter(grad_down_w.astype(jnp.bfloat16), 'wsh', scatter_dimensi...  55.6 us
    reduce_scatter x1, waiting for transfers between devices, on_device(): lax.psum_scatter(grad_up_w.astype(jnp.bfloat16), 'wsh', scatter_dimension...  55.5 us
    all_gather x1, waiting for transfers between devices, on_device(): lax.all_gather(up_weight, 'wsh', axis=0, tiled=True)  50.2 us
    all_gather x1, waiting for transfers between devices, on_device(): group_grads = lax.all_gather(grad_attended, 'ctx', axis=0, tiled=True)  42.9 us
    all_gather x1, waiting for transfers between devices, on_device(): lax.all_gather(down_weight, 'wsh', axis=0, tiled=True)  32.7 us
  transfers between devices with their start and end apart: 13, of which 13 were waited for; matrix products, arithmetic and copies ran while one was open for 10% of the time, Pallas kernels for 0%

commit v1 on v0

v1 whole, which is shorter than its diff:
```python
import jax
import jax.numpy as jnp
from jax import lax
from jax.sharding import PartitionSpec as P

HEAD_DIM = 64
CLUSTER = 128


epsilon = 1e-05


def inner(left, right):
    return lax.dot_general(
        left, right, (((0,), (0,)), ((), ())), preferred_element_type=jnp.float32
    )


def times_transposed(left, right):
    return lax.dot_general(
        left, right, (((1,), (1,)), ((), ())), preferred_element_type=jnp.float32
    )


def normalize(values):
    centre = values - jnp.mean(values, axis=1, keepdims=True)
    factor = lax.rsqrt(jnp.mean(centre * centre, axis=1, keepdims=True) + epsilon)
    return (centre * factor, factor)


def norm_back(grad_out, normed, factor, gain):
    grad_normed = grad_out * gain
    return factor * (
        grad_normed
        - jnp.mean(grad_normed, axis=1, keepdims=True)
        - normed * jnp.mean(grad_normed * normed, axis=1, keepdims=True)
    )


def on_device(
    tokens,
    cluster_order,
    qkv_weight,
    query_bias,
    value_bias,
    out_weight,
    out_bias,
    first_gain,
    first_shift,
    up_weight,
    up_bias,
    down_weight,
    down_bias,
    second_gain,
    second_shift,
    cotangent,
):
    order = cluster_order[0]
    rows = tokens.shape[1]
    width = tokens.shape[2]
    heads = width // HEAD_DIM
    blocks = rows // CLUSTER
    group_rows = rows * lax.axis_size("ctx")
    first_row = lax.axis_index("ctx") * rows
    factor_qk = HEAD_DIM ** (-0.5)
    small = [
        query_bias,
        value_bias,
        out_bias,
        first_gain,
        first_shift,
        down_bias,
        second_gain,
        second_shift,
        up_bias,
    ]
    sizes = [v.shape[0] for v in small]
    packed = lax.all_gather(jnp.concatenate(small), "wsh", axis=0, tiled=False)
    spots = [sum(sizes[:i]) for i in range(len(sizes))]
    (qbias, vbias, obias, gain_one, shift_one, dbias, gain_two, shift_two, ubias) = [
        packed[:, s : s + n].reshape(-1).astype(jnp.float32) for s, n in zip(spots, sizes)
    ]
    whole_order = lax.all_gather(order, "ctx", axis=0, tiled=True)
    both = lax.all_gather(
        jnp.concatenate([tokens[0], cotangent[0]], axis=1), "ctx", axis=0, tiled=True
    )
    whole_qkv = lax.all_gather(qkv_weight, "wsh", axis=0, tiled=True)
    whole_out = lax.all_gather(out_weight, "wsh", axis=0, tiled=True)
    whole_up = lax.all_gather(up_weight, "wsh", axis=0, tiled=True)
    whole_down = lax.all_gather(down_weight, "wsh", axis=0, tiled=True)
    take = (order[:, None] == jnp.arange(group_rows, dtype=jnp.int32)[None, :]).astype(jnp.bfloat16)
    home = (
        (first_row + jnp.arange(rows, dtype=jnp.int32))[:, None] == whole_order[None, :]
    ).astype(jnp.bfloat16)
    mine = jnp.dot(take, both, preferred_element_type=jnp.float32)
    inputs = mine[:, :width].astype(jnp.bfloat16)
    grad_top = mine[:, width:]
    qkv_shift = jnp.concatenate([qbias, jnp.zeros((width,), jnp.float32), vbias])
    own_qkv = (jnp.dot(inputs, whole_qkv, preferred_element_type=jnp.float32) + qkv_shift).astype(
        jnp.bfloat16
    )
    query = own_qkv[:, :width].reshape(blocks, CLUSTER, heads, HEAD_DIM)
    keyed = own_qkv[:, width : 2 * width].reshape(blocks, CLUSTER, heads, HEAD_DIM)
    valued = own_qkv[:, 2 * width :].reshape(blocks, CLUSTER, heads, HEAD_DIM)
    places = order.reshape(blocks, CLUSTER)
    visible = (places[:, None, :] <= places[:, :, None])[:, None, :, :]
    scores = (
        jnp.einsum("cihd,cjhd->chij", query, keyed, preferred_element_type=jnp.float32) * factor_qk
    )
    masked = jnp.where(visible, scores, -1e30)
    row_max = jnp.max(masked, axis=3, keepdims=True)
    expd = jnp.where(visible, jnp.exp(masked - row_max), 0.0)
    total = jnp.sum(expd, axis=3, keepdims=True)
    probs_full = expd / total
    probs = probs_full.astype(jnp.bfloat16)
    context = (
        jnp.einsum("chij,cjhd->cihd", probs, valued, preferred_element_type=jnp.float32)
        .astype(jnp.bfloat16)
        .reshape(rows, width)
    )
    attended = (
        (jnp.dot(context, whole_out, preferred_element_type=jnp.float32) + obias)
        .astype(jnp.bfloat16)
        .astype(jnp.float32)
    )
    resid = inputs.astype(jnp.float32) + attended
    first_norm, first_factor = normalize(resid)
    first_out = first_norm * gain_one + shift_one
    first_low = first_out.astype(jnp.bfloat16)
    pre_act = jnp.dot(first_low, whole_up, preferred_element_type=jnp.float32) + ubias
    half = 0.5 * (1.0 + lax.erf(pre_act * 0.7071067811865476))
    hidden = (pre_act * half).astype(jnp.bfloat16)
    slope = half + pre_act * jnp.exp(-0.5 * pre_act * pre_act) * 0.3989422804014327
    second_in = first_out + jnp.dot(hidden, whole_down, preferred_element_type=jnp.float32) + dbias
    second_norm, second_factor = normalize(second_in)
    layer_out = (second_norm * gain_two + shift_two).astype(jnp.bfloat16)
    group_out = lax.all_gather(layer_out, "ctx", axis=0, tiled=True)
    out_home = jnp.dot(home, group_out, preferred_element_type=jnp.float32).astype(jnp.bfloat16)
    grad_gain_two = jnp.sum(grad_top * second_norm, axis=0)
    grad_shift_two = jnp.sum(grad_top, axis=0)
    grad_second = norm_back(grad_top, second_norm, second_factor, gain_two)
    grad_branch2 = grad_second.astype(jnp.bfloat16)
    grad_down_w = inner(hidden, grad_branch2).astype(jnp.bfloat16)
    grad_down_b = jnp.sum(grad_branch2.astype(jnp.float32), axis=0)
    grad_hidden = times_transposed(grad_branch2, whole_down)
    grad_pre = (grad_hidden * slope).astype(jnp.bfloat16)
    grad_up_w = inner(first_low, grad_pre).astype(jnp.bfloat16)
    grad_up_b = jnp.sum(grad_pre.astype(jnp.float32), axis=0)
    grad_first = grad_second + times_transposed(grad_pre, whole_up)
    grad_gain_one = jnp.sum(grad_first * first_norm, axis=0)
    grad_shift_one = jnp.sum(grad_first, axis=0)
    grad_resid = norm_back(grad_first, first_norm, first_factor, gain_one)
    grad_attended = grad_resid.astype(jnp.bfloat16)
    grad_out_b = jnp.sum(grad_attended.astype(jnp.float32), axis=0)
    grad_out_w = inner(context, grad_attended).astype(jnp.bfloat16)
    grad_context = (
        times_transposed(grad_attended, whole_out)
        .astype(jnp.bfloat16)
        .reshape(blocks, CLUSTER, heads, HEAD_DIM)
    )
    grad_probs = jnp.einsum(
        "cihd,cjhd->chij", grad_context, valued, preferred_element_type=jnp.float32
    )
    grad_valued = jnp.einsum(
        "chij,cihd->cjhd", probs, grad_context, preferred_element_type=jnp.float32
    ).astype(jnp.bfloat16)
    inner_sum = jnp.sum(probs_full * grad_probs, axis=3, keepdims=True)
    grad_scores = (probs_full * (grad_probs - inner_sum)).astype(jnp.bfloat16)
    grad_query = (
        jnp.einsum("chij,cjhd->cihd", grad_scores, keyed, preferred_element_type=jnp.float32)
        * factor_qk
    ).astype(jnp.bfloat16)
    grad_keyed = (
        jnp.einsum("chij,cihd->cjhd", grad_scores, query, preferred_element_type=jnp.float32)
        * factor_qk
    ).astype(jnp.bfloat16)
    own_grad = jnp.concatenate(
        [
            grad_query.reshape(rows, width),
            grad_keyed.reshape(rows, width),
            grad_valued.reshape(rows, width),
        ],
        axis=1,
    )
    grad_query_b = jnp.sum(own_grad[:, :width].astype(jnp.float32), axis=0)
    grad_value_b = jnp.sum(own_grad[:, 2 * width :].astype(jnp.float32), axis=0)
    grad_qkv_w = inner(inputs, own_grad).astype(jnp.bfloat16)
    grad_inputs = (grad_resid + times_transposed(own_grad, whole_qkv)).astype(jnp.bfloat16)
    group_in = lax.all_gather(grad_inputs, "ctx", axis=0, tiled=True)
    in_home = jnp.dot(home, group_in, preferred_element_type=jnp.float32)

    def summed(grad):
        part = lax.psum_scatter(grad, "wsh", scatter_dimension=0, tiled=True)
        return lax.psum(part, "ctx").astype(jnp.float32)

    sums = [summed(g) for g in (grad_down_w, grad_up_w, grad_out_w, grad_qkv_w)]
    small_grads = [
        grad_query_b,
        grad_value_b,
        grad_out_b,
        grad_gain_one,
        grad_shift_one,
        grad_down_b,
        grad_gain_two,
        grad_shift_two,
        grad_up_b,
    ]
    parts = lax.axis_size("wsh")
    table = jnp.concatenate([g.reshape(parts, -1) for g in small_grads], axis=1)
    table = lax.psum(table, ("ctx", "wsh"))
    own = lax.dynamic_slice_in_dim(table, lax.axis_index("wsh"), 1, 0)[0]
    (g_q, g_v, g_o, g_g1, g_s1, g_d, g_g2, g_s2, g_u) = [
        own[s : s + n] for s, n in zip(spots, sizes)
    ]
    return (
        out_home[None],
        in_home[None],
        sums[3],
        g_q,
        g_v,
        sums[2],
        g_o,
        g_g1,
        g_s1,
        sums[1],
        g_u,
        sums[0],
        g_d,
        g_g2,
        g_s2,
    )


def solution(mesh):
    row = P("wsh", None)
    vec = P("wsh")
    seq = P("wsh", "ctx", None)
    in_specs = (
        seq,
        P("wsh", "ctx"),
        row,
        vec,
        vec,
        row,
        vec,
        vec,
        vec,
        row,
        vec,
        row,
        vec,
        vec,
        vec,
        seq,
    )
    out_specs = (
        seq,
        seq,
        row,
        vec,
        vec,
        row,
        vec,
        vec,
        vec,
        row,
        vec,
        row,
        vec,
        vec,
        vec,
    )
    return jax.shard_map(
        on_device, mesh=mesh, in_specs=in_specs, out_specs=out_specs, check_vma=False
    )
```

time: 825 us -> 663 us (0.80)
  waiting for transfers between devices: 547 us -> 452 us
  local copies, waits for them, and re-layouts: 68.7 us -> 22.8 us
  blocking collectives: 80.7 us -> 61.3 us
    reduce_scatter x5 -> x4, waiting for transfers between devices: 268 us -> 151 us  [summed(): part = lax.psum_scatter(grad, 'wsh', scatter_dimension=0, tiled=True)]
    unnamed x2 -> x0, blocking collectives: 57.6 us -> none
    psum x1, waiting for transfers between devices: 18.7 us -> 63.9 us  [summed(): return lax.psum(part, 'ctx').astype(jnp.float32)]
    psum x1, blocking collectives: 9.97 us -> 37.6 us  [on_device(): table = lax.psum(table, ('ctx', 'wsh'))]
    unnamed x14 -> x12, waiting for transfers between devices: 29.1 us -> 3.23 us
    gather x2 -> x0, local copies, waits for them, and re-layouts: 16.4 us -> none  [the longest x1 10.8 us: on_device(): picked = jnp.take(group_qkv, order, axis=0)]
    scatter x2 -> x0, local copies, waits for them, and re-layouts: 15.4 us -> none  [the longest x1 10.7 us: on_device(): jnp.zeros((group_rows, 3 * width), jnp.bfloat16).at[order].set(grad_picked)]
    unnamed x79 -> x78, local copies, waits for them, and re-layouts: 22 us -> 6.66 us
  transfers between devices with their start and end apart: 13 -> 12, of which waited for: 13 -> 10; matrix products, arithmetic and copies ran while one was open for 10% -> 11% of each run, Pallas kernels for 0% -> 0%
where the time goes in v1:
time: 663 us; the launch traced here: 654 us
  waiting for transfers between devices  452 us (68%)
  matrix products  82.2 us (12%)
  blocking collectives  61.3 us (9%)
  local copies, waits for them, and re-layouts  22.8 us (3%)
  other arithmetic  20.3 us (3%)
  between operations  15.3 us (2%)
    reduce_scatter x4, waiting for transfers between devices, summed(): part = lax.psum_scatter(grad, 'wsh', scatter_dimension=0, tiled=True)  151 us
    psum x1, waiting for transfers between devices, summed(): return lax.psum(part, 'ctx').astype(jnp.float32)  63.9 us
    all_gather x1, waiting for transfers between devices, on_device(): lax.all_gather(jnp.concatenate([tokens[0], cotangent[0]], axis=1), 'ctx',...  53.9 us
    all_gather x1, waiting for transfers between devices, on_device(): whole_up = lax.all_gather(up_weight, 'wsh', axis=0, tiled=True)  48.2 us
    all_gather x1, waiting for transfers between devices, on_device(): whole_down = lax.all_gather(down_weight, 'wsh', axis=0, tiled=True)  43.3 us
    all_gather x1, waiting for transfers between devices, on_device(): group_out = lax.all_gather(layer_out, 'ctx', axis=0, tiled=True)  40.1 us
    psum x1, blocking collectives, on_device(): table = lax.psum(table, ('ctx', 'wsh'))  37.6 us
    all_gather x1, waiting for transfers between devices, on_device(): whole_qkv = lax.all_gather(qkv_weight, 'wsh', axis=0, tiled=True)  37.4 us
  transfers between devices with their start and end apart: 12, of which 10 were waited for; matrix products, arithmetic and copies ran while one was open for 11% of the time, Pallas kernels for 0%

profile of v1, /device:TPU:0, one launch (start us, length us, event | category | flops | bytes accessed | tf_op | source)
XLA Modules:
  0.0 654.4 jit_solution(16202312041115670555)
XLA Ops:
  7.2 2.6 pad_maximum_fusion
  10.0 0.7 all-gather.13.cloned.1.call-update
  10.8 0.7 all-gather.15.cloned.1.call-update
  12.1 0.5 all-gather.19.cloned.1.call-update
  12.8 15.7 %all-gather.2 = bf16[8,1,1152]{2,1,0:T(2,128)(2,1)S(1)} all-gather(bf16[1,1,1152]{2,1,0:T(2,128)(2,1)S(1)} %reshape.237), channel_id=3, replica_groups=mesh['ctx'=4,'wsh'=8] {'wsh'}, dimensions={0}, use_global_device_ids=true | all-gather | bytes 20736 | tf_op jit(solution)/shard_map/all_gather | solution.py:78
  29.4 53.9 %all-gather.11.cloned.1.call-done = bf16[2048,1536]{1,0:T(8,128)(2,1)} async-done(((bf16[512,1536]{1,0:T(8,128)(2,1)}), bf16[2048,1536]{1,0:T(8,128)(2,1)}) %all-gather.11.cloned.1.call-update) | async-done | bytes 6291472 | tf_op jit(solution)/shard_map/all_gather | solution.py:84
  83.3 5.8 fusion.12
  89.2 37.4 %all-gather.13.cloned.1.call-done = bf16[768,2304]{1,0:T(8,128)(2,1)} async-done(((bf16[96,2304]{1,0:T(8,128)(2,1)}), bf16[768,2304]{1,0:T(8,128)(2,1)}) %all-gather.13.cloned.1.call-update) | async-done | bytes 3538960 | tf_op jit(solution)/shard_map/all_gather | solution.py:87
  126.5 4.0 fusion.11
  130.5 1.4 fusion.67
  132.0 1.5 copy.64
  135.1 0.6 fusion.52
  135.7 1.0 fusion.68
  136.8 0.6 fusion.35
  137.4 1.0 copy-done.11
  138.4 0.6 copy.70
  139.0 10.7 %all-gather.15.cloned.1.call-done = bf16[768,768]{1,0:T(8,128)(2,1)} async-done(((bf16[96,768]{1,0:T(8,128)(2,1)}), bf16[768,768]{1,0:T(8,128)(2,1)}) %all-gather.15.cloned.1.call-update) | async-done | bytes 1179664 | tf_op jit(solution)/shard_map/all_gather | solution.py:88
  149.7 2.7 fusion.26
  152.4 2.1 multiply_reduce_fusion.6
  154.5 48.2 %all-gather.17.cloned.1.call-done = bf16[768,3072]{1,0:T(8,128)(2,1)} async-done(((bf16[96,3072]{1,0:T(8,128)(2,1)}), bf16[768,3072]{1,0:T(8,128)(2,1)}) %all-gather.17.cloned.1.call-update) | async-done | bytes 4718608 | tf_op jit(solution)/shard_map/all_gather | solution.py:89
  202.7 8.7 %multiply_convert_fusion = (bf16[512,3072]{1,0:T(8,128)(2,1)}, f32[512,3072]{1,0:T(8,128)}) fusion(f32[3072]{0:T(1024)S(1)} %reshape.231, bf16[768,3072]{1,0:T(8,128)(2,1)} %all-gather.17.cloned.1.call-done, f32[768]{0:T(1024)S(1)} %reshape.230, f32[768]{0:T(1024)S(1)} %reshape.229, f32[512]{0:T(512)S(1)} %add_rsqrt_fusion.1, ...), kind=kOutput, calls=%fused_computation.9 | convolution fusion | flops 2428502016 | bytes 15751168 | tf_op jit(solution)/shard_map/dot_general | solution.py:130
  211.5 43.3 %all-gather.19.cloned.1.call-done = bf16[3072,768]{1,0:T(8,128)(2,1)} async-done(((bf16[384,768]{1,0:T(8,128)(2,1)}), bf16[3072,768]{1,0:T(8,128)(2,1)}) %all-gather.19.cloned.1.call-update) | async-done | bytes 4718608 | tf_op jit(solution)/shard_map/all_gather | solution.py:90
  254.8 6.7 %fusion.69 = (f32[512]{0:T(512)S(1)}, f32[512,768]{1,0:T(8,128)S(1)}) fusion(f32[768]{0:T(1024)S(1)} %reshape.232, bf16[512,3072]{1,0:T(8,128)(2,1)} %get-tuple-element.55, bf16[3072,768]{1,0:T(8,128)(2,1)} %all-gather.19.cloned.1.call-done, f32[768]{0:T(1024)S(1)} %reshape.230, f32[768]{0:T(1024)S(1)} %reshape.229, f32[512]{0:T(512)S(1)} %add_rsqrt_fusion.1, ...), kind=kOutput, calls=%fused_computation.137 | convolution fusion | flops 2419850752 | bytes 11025408 | tf_op jit(solution)/shard_map/dot_general | solution.py:134
  261.8 0.8 multiply_reduce_fusion.1
  262.7 1.5 convert_reduce_fusion.1
  264.2 4.7 convert_reduce_fusion
  269.0 3.2 multiply_reduce_fusion.2
  272.3 1.9 convert_reduce_fusion.2
  274.1 1.7 convolution_convert_fusion.4
  275.9 2.3 copy.71
  278.2 2.6 reshape.213
  280.8 4.4 convert_reduce_fusion.3
  285.2 2.5 multiply_reduce_fusion
  287.7 1.8 convolution_convert_fusion.3
  289.5 2.6 copy.82
  292.2 3.8 multiply_convert_fusion.1
  296.0 1.2 fusion.38
  297.2 0.6 copy.79
  297.8 0.7 convert_reduce_fusion.4
  298.5 0.6 copy.76
  299.7 1.4 copy-done.19
  301.1 0.7 copy-done.2
  301.8 3.9 convolution_convert_fusion.2
  305.8 7.2 %convolution_convert_fusion.1 = bf16[768,3072]{1,0:T(8,128)(2,1)} fusion(bf16[512,3072]{1,0:T(8,128)(2,1)} %copy-done.34, f32[768]{0:T(1024)S(1)} %reshape.230, f32[768]{0:T(1024)S(1)} %reshape.229, bf16[512,768]{1,0:T(8,128)(2,1)} %copy-done.5, f32[512]{0:T(512)S(1)} %add_rsqrt_fusion.1, f32[512]{0:T(512)S(1)} %broadcast_multiply_fusion.5, ...), kind=kOutput, calls=%fused_computation.16 | convolution fusion | flops 2421424128 | bytes 9449472 | tf_op jit(solution)/shard_map/dot_general | solution.py:14
  313.3 1.1 copy-done.14
  314.4 6.7 %convolution_convert_fusion = bf16[3072,768]{1,0:T(8,128)(2,1)} fusion(bf16[512,3072]{1,0:T(8,128)(2,1)} %get-tuple-element.55, f32[512,768]{1,0:T(8,128)S(1)} %copy-done.14), kind=kOutput, calls=%fused_computation.15 | convolution fusion | flops 2418671616 | bytes 9437184 | tf_op jit(solution)/shard_map/dot_general | solution.py:14
  321.2 1.3 copy-done.4
  322.5 5.7 add_convert_fusion
  328.3 0.7 all-gather.21.cloned.1.call-update
  329.0 39.2 %reduce-scatter.5.cloned.1.call-done = bf16[96,2304]{1,0:T(8,128)(2,1)} async-done(((bf16[768,2304]{1,0:T(8,128)(2,1)}), bf16[96,2304]{1,0:T(8,128)(2,1)}) %reduce-scatter.5.cloned.1.call-update) | async-done | bytes 442384 | tf_op jit(solution)/shard_map/reduce_scatter | solution.py:193
  368.2 55.9 %reduce-scatter.9.cloned.1.call-done = bf16[96,3072]{1,0:T(8,128)(2,1)} async-done(((bf16[768,3072]{1,0:T(8,128)(2,1)}), bf16[96,3072]{1,0:T(8,128)(2,1)}) %reduce-scatter.9.cloned.1.call-update) | async-done | bytes 589840 | tf_op jit(solution)/shard_map/reduce_scatter | solution.py:193
  424.1 55.8 %reduce-scatter.11.cloned.1.call-done = bf16[384,768]{1,0:T(8,128)(2,1)} async-done(((bf16[3072,768]{1,0:T(8,128)(2,1)}), bf16[384,768]{1,0:T(8,128)(2,1)}) %reduce-scatter.11.cloned.1.call-update) | async-done | bytes 589840 | tf_op jit(solution)/shard_map/reduce_scatter | solution.py:193
  479.9 8.0 %all-gather = s32[1,2048]{1,0:T(1,128)S(1)} all-gather(s32[1,512]{1,0:T(1,128)S(1)} %copy-done.21), channel_id=2, replica_groups=mesh['ctx'=4,'wsh'=8] {'ctx'}, dimensions={1}, use_global_device_ids=true | all-gather | bytes 10240 | tf_op jit(solution)/shard_map/all_gather | solution.py:83
  488.6 37.6 %psum.36 = f32[8,1152]{1,0:T(8,128)S(1)} all-reduce(f32[8,1152]{1,0:T(8,128)S(1)} %concatenate.19), channel_id=1, replica_groups=mesh['ctx'=4,'wsh'=8] {'ctx','wsh'}, use_global_device_ids=true, to_apply=%region_22.23 | all-reduce | flops 9216 | bytes 73728 | tf_op jit(solution)/shard_map/psum | solution.py:210
  526.2 0.7 dynamic-slice_reduce_fusion
  526.9 0.6 dynamic-slice_bitcast_fusion
  527.5 4.9 fusion.22
  532.3 40.1 %all-gather.21.cloned.1.call-done = bf16[2048,768]{1,0:T(8,128)(2,1)} async-done(((bf16[512,768]{1,0:T(8,128)(2,1)}), bf16[2048,768]{1,0:T(8,128)(2,1)}) %all-gather.21.cloned.1.call-update) | async-done | bytes 3145744 | tf_op jit(solution)/shard_map/all_gather | solution.py:137
  572.5 4.6 fusion.32
  577.1 63.9 %all-reduce.3.cloned.1.call-done = (bf16[96,2304]{1,0:T(8,128)(2,1)}, bf16[96,768]{1,0:T(8,128)(2,1)}, bf16[96,3072]{1,0:T(8,128)(2,1)}, bf16[384,768]{1,0:T(8,128)(2,1)}) async-done(((bf16[96,2304]{1,0:T(8,128)(2,1)}, bf16[96,768]{1,0:T(8,128)(2,1)}, bf16[96,3072]{1,0:T(8,128)(2,1)}, bf16[384,768]{1,0:T(8,128)(2,1)}), (bf16[96,2304]{1,0:T(8,128)(2,1)}, bf16[96,768]{1,0:T(8,128)(2,1)}, ...) | async-done | bytes 1769488 | tf_op jit(solution)/shard_map/psum | solution.py:194
  641.0 2.2 convert_element_type.246
  643.2 2.2 convert_element_type.248
  645.4 1.0 convert_element_type.237
  646.4 0.7 convert_element_type.244
  (136 shorter events, 5.6 us)
Async XLA Ops:
  7.2 76.1 %all-gather.11.cloned.1.call-start = ((), (), s32[]{:S(2)}) async-start(), calls=%async_computation.4 | async-start | bytes 7864320 | tf_op jit(solution)/shard_map/all_gather | solution.py:84
  9.8 2.8 copy-start.22
  9.8 2.8 copy-start.23
  9.9 2.8 copy-start.24
  9.9 2.8 copy-start.25
  9.9 2.8 copy-start.26
  9.9 2.8 copy-start.27
  9.9 2.8 copy-start.28
  9.9 2.8 copy-start.29
  9.9 2.8 copy-start.30
  9.9 19.3 %copy-start.21 = (s32[1,512]{1,0:T(1,128)S(1)}, s32[1,512]{1,0:T(1,128)}, u32[]{:S(2)}) copy-start(s32[1,512]{1,0:T(1,128)} %param.17) | copy-start | bytes 6148
  10.0 116.6 %all-gather.13.cloned.1.call-start = ((), (), s32[]{:S(2)}) async-start(), calls=%async_computation.5 | async-start | bytes 3981312 | tf_op jit(solution)/shard_map/all_gather | solution.py:87
  10.7 139.0 %all-gather.15.cloned.1.call-start = ((), (), s32[]{:S(2)}) async-start(), calls=%async_computation.6 | async-start | bytes 1327104 | tf_op jit(solution)/shard_map/all_gather | solution.py:88
  11.4 191.3 %all-gather.17.cloned.1.call-start = ((), (), s32[]{:S(2)}) async-start(), calls=%async_computation.7 | async-start | bytes 5308416 | tf_op jit(solution)/shard_map/all_gather | solution.py:89
  12.0 242.8 %all-gather.19.cloned.1.call-start = ((), (), s32[]{:S(2)}) async-start(), calls=%async_computation.8 | async-start | bytes 5308416 | tf_op jit(solution)/shard_map/all_gather | solution.py:90
  12.6 316.4 %reduce-scatter.7.cloned.1.call-start = ((), (), s32[]{:S(2)}) async-start(), calls=%async_computation.12 | async-start | bytes 1327104 | tf_op jit(solution)/shard_map/reduce_scatter | solution.py:193
  89.2 41.4 %copy-start = (f32[512,1536]{1,0:T(8,128)}, f32[512,1536]{1,0:T(8,128)S(1)}, u32[]{:S(2)}) copy-start(f32[512,1536]{1,0:T(8,128)S(1)} %fusion.12) | copy-start | bytes 9437188
  132.0 1.7 copy-start.9
  133.5 1.2 copy-start.8
  135.1 1.7 copy-start.15
  136.8 1.6 copy-start.11
  139.0 13.4 %copy-start.6 = (bf16[4,128,12,64]{1,0,3,2:T(4,128)(2,1)}, bf16[4,128,12,64]{1,0,3,2:T(4,128)(2,1)S(1)}, u32[]{:S(2)}) copy-start(bf16[4,128,12,64]{1,0,3,2:T(4,128)(2,1)S(1)} %copy.70) | copy-start | bytes 2359300
  152.4 116.5 %copy-start.5 = (bf16[512,768]{1,0:T(8,128)(2,1)}, bf16[512,768]{1,0:T(8,128)(2,1)S(1)}, u32[]{:S(2)}) copy-start(bf16[512,768]{1,0:T(8,128)(2,1)S(1)} %get-tuple-element.54) | copy-start | bytes 2359300
  254.8 7.0 %copy-start.1 = (f32[512,1536]{1,0:T(8,128)S(1)}, f32[512,1536]{1,0:T(8,128)}, u32[]{:S(2)}) copy-start(f32[512,1536]{1,0:T(8,128)} %copy-done) | copy-start | bytes 9437188
  254.8 9.4 %copy-start.33 = (f32[512,3072]{1,0:T(8,128)S(1)}, f32[512,3072]{1,0:T(8,128)}, u32[]{:S(2)}) copy-start(f32[512,3072]{1,0:T(8,128)} %get-tuple-element.56) | copy-start | bytes 18874372
  261.8 2.4 copy-start.31
  262.6 6.3 slice-start
  264.2 4.8 copy-start.13
  264.2 4.8 slice-start.1
  268.9 3.3 copy-start.34
  272.2 1.9 copy-start.32
  274.1 13.6 %copy-start.3 = (f32[512,768]{1,0:T(8,128)}, f32[512,768]{1,0:T(8,128)S(1)}, u32[]{:S(2)}) copy-start(f32[512,768]{1,0:T(8,128)S(1)} %get-tuple-element.30) | copy-start | bytes 4718596
  280.8 4.4 copy-start.12
  280.8 4.4 copy-start.16
  280.8 4.4 copy-start.17
  285.2 2.5 copy-start.7
  292.2 76.1 %reduce-scatter.5.cloned.1.call-start = ((), (), s32[]{:S(2)}) async-start(), calls=%async_computation.11 | async-start | bytes 3981312 | tf_op jit(solution)/shard_map/reduce_scatter | solution.py:193
  298.5 1.1 copy-start.10
  299.1 2.7 copy-start.2
  299.7 1.4 copy-start.19
  305.8 118.4 %reduce-scatter.9.cloned.1.call-start = ((), (), s32[]{:S(2)}) async-start(), calls=%async_computation.13 | async-start | bytes 5308416 | tf_op jit(solution)/shard_map/reduce_scatter | solution.py:193
  313.0 1.4 copy-start.14
  313.0 166.9 %reduce-scatter.11.cloned.1.call-start = ((), (), s32[]{:S(2)}) async-start(), calls=%async_computation.14 | async-start | bytes 5308416 | tf_op jit(solution)/shard_map/reduce_scatter | solution.py:193
  321.1 1.4 copy-start.4
  321.1 206.3 %all-gather.23.cloned.1.call-start = ((), (), s32[]{:S(2)}) async-start(), calls=%async_computation.10 | async-start | bytes 3932160 | tf_op jit(solution)/shard_map/all_gather | solution.py:189
  328.2 244.2 %all-gather.21.cloned.1.call-start = ((), (), s32[]{:S(2)}) async-start(), calls=%async_computation.9 | async-start | bytes 3932160 | tf_op jit(solution)/shard_map/all_gather | solution.py:137
  329.0 312.0 %all-reduce.3.cloned.1.call-start = ((), (), s32[]{:S(2)}) async-start(), calls=%async_computation.15 | async-start | bytes 3538944 | tf_op jit(solution)/shard_map/psum | solution.py:194
  641.0 4.4 copy-start.18
  641.0 5.4 copy-start.20
Sparse Core Ops, SparseCore 0:
  10.4 72.8 all-gather.10
  85.0 41.5 all-gather.12
  128.2 21.5 all-gather.14
  151.2 51.4 all-gather.16
  204.2 50.5 all-gather.18
  292.3 31.3 reduce-scatter.6
  326.0 42.1 reduce-scatter.4
  370.6 53.4 reduce-scatter.8
  426.5 53.3 reduce-scatter.10
  482.3 43.4 all-gather.22
  528.3 44.0 all-gather.20
  576.2 64.7 all-reduce.2

commit v2 on v1

v2 whole, which is shorter than its diff:
```python
import functools

import jax
import jax.numpy as jnp
from jax import lax
from jax.experimental import pallas as pl
from jax.experimental.pallas import tpu as pltpu
from jax.sharding import PartitionSpec as P

HEAD_DIM = 64
CLUSTER = 128
LANES = 128
STEP = 256

epsilon = 1e-05
bf16 = jnp.bfloat16
f32 = jnp.float32


def mm(left, right):
    return lax.dot_general(left, right, (((1,), (0,)), ((), ())), preferred_element_type=f32)


def mm_nt(left, right):
    return lax.dot_general(left, right, (((1,), (1,)), ((), ())), preferred_element_type=f32)


def mm_tn(left, right):
    return lax.dot_general(left, right, (((0,), (0,)), ((), ())), preferred_element_type=f32)


def flip(index, offset):
    bit = 1
    result = index
    while bit <= offset:
        if offset & bit:
            result = result + bit * (1 - 2 * ((index // bit) % 2))
        bit *= 2
    return result


def bits_of(size):
    found, bit = [], 1
    while bit < size:
        found.append(bit)
        bit *= 2
    return found


def low_bit(value):
    return value & -value


class Flight:
    def __init__(self, copy):
        self.copy, self.leaving = copy, True
        copy.start()

    def wait_recv(self):
        self.copy.wait_recv()

    def wait_send(self):
        if self.leaving:
            self.copy.wait_send()
        self.leaving = False


class Links:
    def __init__(self, send_sem, recv_sem):
        self.send_sem, self.recv_sem, self.used = send_sem, recv_sem, 0
        self.sent = []

    def send(self, src, dst, ctx, wsh):
        n = self.used
        self.used += 1
        flight = Flight(
            pltpu.make_async_remote_copy(
                src_ref=src,
                dst_ref=dst,
                send_sem=self.send_sem.at[n],
                recv_sem=self.recv_sem.at[n],
                device_id=(ctx, wsh),
                device_id_type=pl.DeviceIdType.MESH,
            )
        )
        self.sent.append(flight)
        return flight

    def local(self, src, dst):
        n = self.used
        self.used += 1
        copy = pltpu.make_async_copy(src, dst, self.send_sem.at[n])
        copy.start()
        return copy

    def drain(self):
        for copy in self.sent:
            copy.wait_send()
        self.sent = []


class CtxGather:
    def __init__(self, links, own, buffer, ctx, wsh, count, halves):
        self.links, self.own, self.buffer, self.ctx, self.wsh = links, own, buffer, ctx, wsh
        rows = buffer.shape[1] // halves
        self.spans = [pl.ds(h * rows, rows) for h in range(halves)]
        order = bits_of(count)
        self.orders = [order, order[1::-1] + order[2:]][:halves]
        self.have = [{0: None} for _ in self.spans]
        self.step = 0
        self.steps = len(order)

    def advance(self):
        for h, span in enumerate(self.spans):
            bit = self.orders[h][self.step]
            new = {}
            for offset, arrival in self.have[h].items():
                if arrival is not None:
                    arrival.wait_recv()
                    self.have[h][offset] = None
                block = flip(self.ctx, offset)
                src = self.own.at[span] if offset == 0 else self.buffer.at[block, span]
                new[offset ^ bit] = self.links.send(
                    src, self.buffer.at[block, span], flip(self.ctx, bit), self.wsh
                )
            self.have[h].update(new)
        self.step += 1

    def need(self, offset):
        for have in self.have:
            if have[offset] is not None:
                have[offset].wait_recv()
                have[offset] = None


class WeightGather:
    def __init__(self, links, shard, whole, place, sizes, pair):
        self.links, self.shard, self.whole = links, shard, whole
        self.ctx, self.z, self.core = place
        self.zs = sizes
        self.pair = pair
        self.rows, self.columns = shard.shape
        self.bits = bits_of(sizes)[::-1]

    def row_span(self, offset, core):
        first = (flip(self.z, offset) * 2 + core) * self.rows
        return pl.ds(pl.multiple_of(first, 16), self.rows)

    def column_span(self, mine):
        if self.pair is None:
            return pl.ds(0, self.columns)
        half = self.columns // 2
        side = (self.ctx // self.pair) % 2
        if not mine:
            side = 1 - side
        return pl.ds(pl.multiple_of(side * half, LANES), half)

    def wsh_of(self, offset, core):
        return flip(self.z, offset) * 2 + core

    def start(self):
        span = self.column_span(True)
        rows = self.row_span(0, self.core)
        self.from_z, self.from_pair, self.from_core = {}, {}, []
        for bit in self.bits:
            self.from_z[bit] = self.links.send(
                self.shard.at[:, span],
                self.whole.at[rows, span],
                self.ctx,
                self.wsh_of(bit, self.core),
            )
        self.from_core.append(
            self.links.send(
                self.shard, self.whole.at[rows], self.ctx, self.wsh_of(0, 1 - self.core)
            )
        )
        self.own = self.links.local(self.shard, self.whole.at[rows])

    def to_core(self, offset, span):
        part = self.whole.at[self.row_span(offset, self.core), span]
        self.from_core.append(
            self.links.send(part, part, self.ctx, self.wsh_of(0, 1 - self.core))
        )

    def take_z(self):
        span = self.column_span(True)
        for offset in sorted(range(1, self.zs), key=lambda o: (-low_bit(o), o)):
            self.from_z[offset].wait_recv()
            part = self.whole.at[self.row_span(offset, self.core), span]
            for bit in self.bits:
                if bit < low_bit(offset):
                    self.from_z[offset + bit] = self.links.send(
                        part, part, self.ctx, self.wsh_of(bit, self.core)
                    )
            if self.pair is not None:
                self.from_pair[offset] = self.links.send(
                    part, part, flip(self.ctx, self.pair), self.wsh_of(0, self.core)
                )
            self.to_core(offset, span)

    def take_pair(self):
        if self.pair is None:
            return
        span = self.column_span(False)
        for offset, arrival in self.from_pair.items():
            arrival.wait_recv()
            self.to_core(offset, span)

    def finish(self):
        self.own.wait()
        for arrival in self.from_core:
            arrival.wait_recv()


class GradScatter:
    def __init__(self, links, whole, from_core, from_z, from_ctx, place, zs, ctxs):
        self.links, self.whole = links, whole
        self.from_core, self.from_z, self.from_ctx = from_core, from_z, from_ctx
        self.ctx, self.z, self.core = place
        self.zs, self.ctxs = zs, ctxs
        self.rows = whole.shape[0] // (2 * zs)
        self.zbits, self.cbits = bits_of(zs), bits_of(ctxs)
        self.order = sorted(range(zs), key=lambda o: -(o % 2))

    def span(self, offset, core):
        first = (flip(self.z, offset) * 2 + core) * self.rows
        return pl.ds(pl.multiple_of(first, 16), self.rows)

    def send_core(self):
        self.arrive = {}
        for offset in self.order:
            self.arrive[offset] = self.links.send(
                self.whole.at[self.span(offset, 1 - self.core)],
                self.from_core.at[offset],
                self.ctx,
                self.z * 2 + 1 - self.core,
            )

    def add(self, offset, other):
        first = (flip(self.z, offset) * 2 + self.core) * self.rows
        columns = self.whole.shape[1]
        piece = 48 if columns <= 768 else 16

        def body(i, carry):
            here = pl.ds(pl.multiple_of(first + i * piece, 16), piece)
            there = pl.ds(pl.multiple_of(i * piece, 16), piece)
            self.whole[here, :] = (
                self.whole[here, :].astype(f32) + other[there, :].astype(f32)
            ).astype(bf16)
            return carry

        lax.fori_loop(0, self.rows // piece, body, 0)

    def add_core(self):
        for offset in self.order:
            self.arrive[offset].wait_recv()
            self.add(offset, self.from_core.at[offset])

    def z_slot(self, bit, offset):
        first = 0
        for earlier in self.zbits:
            if earlier == bit:
                break
            first += self.zs // (2 * earlier)
        return first + offset // (2 * bit)

    def send_z(self, bit):
        self.arrive = {}
        for offset in range(bit, self.zs, 2 * bit):
            self.arrive[offset - bit] = self.links.send(
                self.whole.at[self.span(offset, self.core)],
                self.from_z.at[self.z_slot(bit, offset - bit)],
                self.ctx,
                flip(self.z, bit) * 2 + self.core,
            )

    def add_z(self, bit):
        for offset, arrival in self.arrive.items():
            arrival.wait_recv()
            self.add(offset, self.from_z.at[self.z_slot(bit, offset)])

    def send_ctx(self, bit):
        self.arrive = self.links.send(
            self.whole.at[self.span(0, self.core)],
            self.from_ctx.at[self.cbits.index(bit)],
            flip(self.ctx, bit),
            self.z * 2 + self.core,
        )

    def add_ctx(self, bit):
        self.arrive.wait_recv()
        self.arrive.wait_send()
        self.add(0, self.from_ctx.at[self.cbits.index(bit)])

    def steps(self):
        self.add_core()
        for bit in self.zbits:
            self.send_z(bit)
            yield
            self.add_z(bit)
        for bit in self.cbits:
            self.send_ctx(bit)
            yield
            self.add_ctx(bit)
        yield


class TableSum:
    def __init__(self, links, table, slots, place, zs, ctxs):
        self.links, self.table, self.slots = links, table, slots
        self.ctx, self.z, self.core = place
        self.hops = (
            [(self.ctx, self.z * 2 + 1 - self.core)]
            + [(self.ctx, flip(self.z, b) * 2 + self.core) for b in bits_of(zs)]
            + [(flip(self.ctx, b), self.z * 2 + self.core) for b in bits_of(ctxs)]
        )

    def steps(self):
        for n, (ctx, wsh) in enumerate(self.hops):
            copy = self.links.send(self.table, self.slots.at[n], ctx, wsh)
            yield
            copy.wait_recv()
            copy.wait_send()
            self.table[...] = self.table[...] + self.slots[n]
        yield


def layer_kernel(
    ctxs,
    zs,
    pairs,
    tok,
    cot,
    order_column,
    order_row,
    vectors,
    qkv_shard,
    out_shard,
    up_shard,
    down_shard,
    home_out,
    home_grad,
    sum_qkv,
    sum_out,
    sum_up,
    sum_down,
    sum_small,
    all_tok,
    all_cot,
    all_out,
    all_grad,
    all_order,
    all_vectors,
    w_qkv,
    w_out,
    w_up,
    w_down,
    g_down,
    stage,
    acc,
    inputs,
    low,
    top,
    qkv,
    probs,
    context,
    turned,
    first_norm,
    first_factor,
    hidden,
    slope,
    grad_wide,
    grad_low,
    result_low,
    back_low,
    rows_768,
    row_up,
    small,
    small_slots,
    core_qkv,
    core_out,
    core_up,
    core_down,
    z_qkv,
    z_out,
    z_up,
    z_down,
    c_qkv,
    c_out,
    c_up,
    c_down,
    send_sem,
    recv_sem,
):
    rows, width = tok.shape
    wide = up_shard.shape[1]
    pairs_of_heads = width // LANES
    blocks = rows // CLUSTER
    scale = HEAD_DIM**-0.5
    ctx = lax.axis_index("ctx")
    wsh = lax.axis_index("wsh")
    z, core = wsh // 2, wsh % 2
    place = (ctx, z, core)
    links = Links(send_sem, recv_sem)

    barrier = pltpu.get_barrier_semaphore()
    peers = (
        [(ctx, z * 2 + 1 - core)]
        + [(ctx, flip(z, b) * 2 + core) for b in bits_of(zs)]
        + [(flip(ctx, b), wsh) for b in bits_of(ctxs)]
    )
    for peer in peers:
        pl.semaphore_signal(barrier, 1, device_id=peer, device_id_type=pl.DeviceIdType.MESH)
    pl.semaphore_wait(barrier, len(peers))

    tok_gather = CtxGather(links, tok, all_tok, ctx, wsh, ctxs, 2)
    cot_gather = CtxGather(links, cot, all_cot, ctx, wsh, ctxs, 2)
    order_gather = CtxGather(links, order_row, all_order, ctx, wsh, ctxs, 1)
    tok_gather.advance()
    order_gather.advance()
    vec_own = links.local(vectors, all_vectors.at[wsh])
    vec_first = links.send(vectors, all_vectors.at[wsh], ctx, z * 2 + 1 - core)
    gathers = [
        WeightGather(links, s, w, place, zs, p)
        for s, w, p in zip(
            (qkv_shard, out_shard, up_shard, down_shard), (w_qkv, w_out, w_up, w_down), pairs
        )
    ]
    for gather in gathers:
        gather.start()

    vec_own.wait()
    vec_first.wait_recv()
    have = 2
    for bit in bits_of(zs):
        span = pl.ds((wsh // have) * have, have)
        copy = links.send(all_vectors.at[span], all_vectors.at[span], ctx, flip(z, bit) * 2 + core)
        copy.wait_recv()
        have *= 2
    while tok_gather.step < tok_gather.steps:
        tok_gather.advance()
        order_gather.advance()

    rows_768[...] = jnp.zeros_like(rows_768)
    row_up[...] = jnp.zeros_like(row_up)
    length = width // (2 * zs)

    def spread(part, row, spot, target, target_row):
        first = min(spot // LANES * LANES, target.shape[1] - STEP)
        j = lax.broadcasted_iota(jnp.int32, (LANES, STEP), 0)
        col = lax.broadcasted_iota(jnp.int32, (LANES, STEP), 1)
        move = jnp.where((col == j + (spot - first)) & (j < length), 1.0, 0.0).astype(bf16)
        moved = mm(part, move)
        n = 8 if row is None else 1
        at = 0 if row is None else row
        where_to = pl.ds(target_row, n), pl.ds(first, STEP)
        target[where_to] = target[where_to] + moved[at : at + n]

    for s in range(2 * zs):
        part = all_vectors[s]
        spread(part, None, length * s, rows_768, 0)
        for r in range(4):
            spread(part, 8 + r, length * (4 * s + r), row_up, 0)

    def pick(gather, own, total):
        copies = {}

        def fetch(offset):
            if offset == 0:
                src = own
            else:
                gather.need(offset)
                src = gather.buffer.at[flip(ctx, offset)]
            copies[offset] = links.local(src, stage.at[offset % 2])

        fetch(0)
        for offset in range(ctxs):
            copies[offset].wait()
            if offset + 1 < ctxs:
                fetch(offset + 1)
            first = flip(ctx, offset) * rows

            def body(i, carry):
                here = pl.ds(pl.multiple_of(i * CLUSTER, CLUSTER), CLUSTER)
                place_of = order_column[here, :]
                lane = lax.broadcasted_iota(jnp.int32, (CLUSTER, LANES), 1)
                chosen = jnp.concatenate(
                    [
                        jnp.where(place_of == lane + (first + t * LANES), 1.0, 0.0).astype(bf16)
                        for t in range(rows // LANES)
                    ],
                    axis=1,
                )
                got = mm(chosen, stage[offset % 2])
                total[here, :] = got if offset == 0 else total[here, :] + got
                return carry

            lax.fori_loop(0, blocks, body, 0)

    def bring_home(gather, own, target):
        copies = {}

        def fetch(offset):
            if offset == 0:
                src = own
            else:
                gather.need(offset)
                src = gather.buffer.at[flip(ctx, offset)]
            copies[offset] = links.local(src, stage.at[offset % 2])

        fetch(0)
        for offset in range(ctxs):
            copies[offset].wait()
            if offset + 1 < ctxs:
                fetch(offset + 1)
            if offset == 0:
                places = order_row[...]
            else:
                order_gather.need(offset)
                places = all_order[flip(ctx, offset)]

            def body(i, carry):
                here = pl.ds(pl.multiple_of(i * CLUSTER, CLUSTER), CLUSTER)
                token = lax.broadcasted_iota(jnp.int32, (CLUSTER, rows), 0) + (
                    ctx * rows + i * CLUSTER
                )
                chosen = jnp.where(places[0:1, :] == token, 1.0, 0.0).astype(bf16)
                got = mm(chosen, stage[offset % 2])
                if offset > 0:
                    got = acc[here, :] + got
                if offset == ctxs - 1:
                    target[here, :] = got.astype(bf16)
                else:
                    acc[here, :] = got
                return carry

            lax.fori_loop(0, blocks, body, 0)

    def tiles(columns, body):
        def step(t, carry):
            body(t, pl.ds(pl.multiple_of(t * STEP, STEP), STEP))
            return carry

        lax.fori_loop(0, columns // STEP, step, 0)

    def row_pass(size, body):
        def step(i, carry):
            body(pl.ds(pl.multiple_of(i * size, size), size))
            return carry

        lax.fori_loop(0, rows // size, step, 0)

    def tally(vector, values):
        total = jnp.sum(values, axis=0, keepdims=True)
        for t in range(width // STEP):
            at = pl.ds(vector * (width // STEP) + t, 1)
            small[at, :] = small[at, :] + total[:, t * STEP : (t + 1) * STEP]

    small[...] = jnp.zeros_like(small)
    qbias, vbias, obias, gain1, shift1, dbias, gain2, shift2 = [
        rows_768.at[pl.ds(n, 1)] for n in range(8)
    ]

    gathers[0].take_z()
    pick(tok_gather, tok, acc)

    def keep_inputs(here):
        inputs[here, :] = acc[here, :].astype(bf16)

    row_pass(CLUSTER, keep_inputs)
    gathers[1].take_z()
    gathers[0].take_pair()
    gathers[1].take_pair()
    cot_gather.advance()
    gathers[0].finish()

    def project(t, span):
        at = pl.ds(pl.multiple_of((t % (width // STEP)) * STEP, STEP), STEP)
        part = t // (width // STEP)
        bias = jnp.where(part == 0, qbias[:, at], jnp.where(part == 2, vbias[:, at], 0.0))
        qkv[:, span] = (mm(inputs[...], w_qkv[:, span]) + bias).astype(bf16)

    tiles(3 * width, project)

    gathers[2].take_z()

    lane = lax.broadcasted_iota(jnp.int32, (1, LANES), 1)
    left = jnp.where(lane < HEAD_DIM, 1.0, 0.0).astype(bf16)
    right = jnp.where(lane < HEAD_DIM, 0.0, 1.0).astype(bf16)

    def both(values):
        return jnp.concatenate([values * left, values * right], axis=0)

    def side_by_side(values):
        return jnp.concatenate([values[:CLUSTER], values[CLUSTER:]], axis=1)

    def part_of(here, kind, pair):
        return qkv[here, kind * width + pair * LANES : kind * width + (pair + 1) * LANES]

    def attend(b, carry):
        here = pl.ds(pl.multiple_of(b * CLUSTER, CLUSTER), CLUSTER)
        visible = order_row[0:1, here] <= order_column[here, :]
        hide = jnp.where(visible, 0.0, -1e30)
        hide = jnp.concatenate([hide, hide], axis=0)
        for pair in range(pairs_of_heads):
            query, keyed, valued = [part_of(here, kind, pair) for kind in range(3)]
            scores = mm_nt(both(query), keyed) * scale + hide
            expd = jnp.exp(scores - jnp.max(scores, axis=1, keepdims=True))
            prob = expd * (1.0 / jnp.sum(expd, axis=1, keepdims=True))
            probs[b * pairs_of_heads + pair] = prob
            got = mm(side_by_side(prob.astype(bf16)), both(valued))
            context[here, pair * LANES : (pair + 1) * LANES] = got.astype(bf16)
        return carry

    lax.fori_loop(0, blocks, attend, 0)
    gathers[2].take_pair()
    gathers[3].take_z()
    while cot_gather.step < cot_gather.steps:
        cot_gather.advance()
    gathers[1].finish()

    def out_project(t, span):
        acc[:, span] = mm(context[...], w_out[:, span])

    tiles(width, out_project)

    def first_normalize(here):
        attended = (acc[here, :] + obias[...]).astype(bf16).astype(f32)
        resid = inputs[here, :].astype(f32) + attended
        centre = resid - jnp.mean(resid, axis=1, keepdims=True)
        factor = lax.rsqrt(jnp.mean(centre * centre, axis=1, keepdims=True) + epsilon)
        normed = centre * factor
        first_norm[here, :] = normed
        first_factor[here, :] = factor
        low[here, :] = (normed * gain1[...] + shift1[...]).astype(bf16)

    row_pass(64, first_normalize)
    pick(cot_gather, cot, acc)

    def keep_top(here):
        top[here, :] = acc[here, :].astype(bf16)

    row_pass(CLUSTER, keep_top)
    gathers[3].take_pair()
    gathers[2].finish()

    def feed(t, span):
        pre = mm(low[...], w_up[:, span]) + row_up[0:1, span]
        half = 0.5 * (1.0 + lax.erf(pre * 0.7071067811865476))
        hidden[:, span] = (pre * half).astype(bf16)
        slope[:, span] = (half + pre * jnp.exp(-0.5 * pre * pre) * 0.3989422804014327).astype(bf16)

    tiles(wide, feed)
    gathers[3].finish()

    def down(t, span):
        acc[:, span] = mm(hidden[...], w_down[:, span])

    tiles(width, down)

    def second_normalize(here):
        first_out = first_norm[here, :] * gain1[...] + shift1[...]
        second_in = first_out + acc[here, :] + dbias[...]
        centre = second_in - jnp.mean(second_in, axis=1, keepdims=True)
        factor = lax.rsqrt(jnp.mean(centre * centre, axis=1, keepdims=True) + epsilon)
        normed = centre * factor
        result_low[here, :] = (normed * gain2[...] + shift2[...]).astype(bf16)
        grad_top = top[here, :].astype(f32)
        tally(6, grad_top * normed)
        tally(7, grad_top)
        grad_normed = grad_top * gain2[...]
        grad = factor * (
            grad_normed
            - jnp.mean(grad_normed, axis=1, keepdims=True)
            - normed * jnp.mean(grad_normed * normed, axis=1, keepdims=True)
        )
        grad_wide[here, :] = grad
        grad = grad.astype(bf16)
        grad_low[here, :] = grad
        tally(5, grad.astype(f32))

    row_pass(64, second_normalize)

    scatters = [
        GradScatter(links, w, a, b, c, place, zs, ctxs)
        for w, a, b, c in (
            (w_qkv, core_qkv, z_qkv, c_qkv),
            (w_out, core_out, z_out, c_out),
            (w_up, core_up, z_up, c_up),
            (g_down, core_down, z_down, c_down),
        )
    ]
    out_gather = CtxGather(links, result_low, all_out, ctx, wsh, ctxs, 2)
    part_rows = wide // (2 * zs)

    def down_grad(owner):
        def body(i, carry):
            here = pl.ds(pl.multiple_of((i * 2 + owner) * part_rows, LANES // 2), part_rows)
            turned_hidden = hidden_turned(i * 2 + owner)
            g_down[here, :] = mm(turned_hidden, grad_low[...]).astype(bf16)
            return carry

        lax.fori_loop(0, zs, body, 0)

    if part_rows % LANES == 0:

        def hidden_turned(s):
            return hidden[:, pl.ds(pl.multiple_of(s * part_rows, LANES), part_rows)].T

        down_grad(1 - core)
        scatters[3].send_core()
        down_grad(core)
    else:

        def all_down(t, span):
            g_down[span, :] = mm(hidden[:, span].T, grad_low[...]).astype(bf16)

        tiles(wide, all_down)
        scatters[3].send_core()
    out_gather.advance()

    def back_hidden(t, span):
        grad = (mm_nt(grad_low[...], w_down[span, :]) * slope[:, span]).astype(bf16)
        slope[:, span] = grad
        small[pl.ds(8 * (width // STEP) + t, 1), :] = jnp.sum(
            grad.astype(f32), axis=0, keepdims=True
        )

    tiles(wide, back_hidden)
    down_steps = scatters[3].steps()
    next(down_steps)

    def back_up(t, span):
        acc[:, span] = mm_nt(slope[...], w_up[span, :])

    tiles(width, back_up)

    def first_back(here):
        grad_first = grad_wide[here, :] + acc[here, :]
        normed = first_norm[here, :]
        tally(3, grad_first * normed)
        tally(4, grad_first)
        grad_normed = grad_first * gain1[...]
        grad = first_factor[here, :] * (
            grad_normed
            - jnp.mean(grad_normed, axis=1, keepdims=True)
            - normed * jnp.mean(grad_normed * normed, axis=1, keepdims=True)
        )
        grad_wide[here, :] = grad
        grad = grad.astype(bf16)
        grad_low[here, :] = grad
        tally(2, grad.astype(f32))

    row_pass(64, first_back)
    while out_gather.step < out_gather.steps:
        out_gather.advance()
    links.drain()

    turned[...] = low[...].T

    def up_grad(t, span):
        w_up[:, span] = mm(turned[...], slope[:, span]).astype(bf16)

    tiles(wide, up_grad)
    scatters[2].send_core()

    turned[...] = context[...].T

    def back_context(t, span):
        context[:, span] = mm_nt(grad_low[...], w_out[span, :]).astype(bf16)

    tiles(width, back_context)

    def out_grad(t, span):
        w_out[:, span] = mm(turned[...], grad_low[:, span]).astype(bf16)

    tiles(width, out_grad)
    scatters[1].send_core()
    up_steps = scatters[2].steps()
    next(up_steps)
    next(down_steps)
    out_steps = scatters[1].steps()
    next(out_steps)

    def back_attend(b, carry):
        here = pl.ds(pl.multiple_of(b * CLUSTER, CLUSTER), CLUSTER)
        for pair in range(pairs_of_heads):
            query, keyed, valued = [part_of(here, kind, pair) for kind in range(3)]
            prob = probs[b * pairs_of_heads + pair]
            grad = both(context[here, pair * LANES : (pair + 1) * LANES])
            grad_prob = mm_nt(grad, valued)
            grad_valued = mm_tn(prob.astype(bf16), grad)
            inner = jnp.sum(prob * grad_prob, axis=1, keepdims=True)
            grad_score = (prob * (grad_prob - inner)).astype(bf16)
            grad_query = mm(side_by_side(grad_score), both(keyed)) * scale
            grad_keyed = mm_tn(grad_score, both(query)) * scale
            for kind, value in enumerate((grad_query, grad_keyed, grad_valued)):
                at = kind * width + pair * LANES
                qkv[here, at : at + LANES] = value.astype(bf16)
        return carry

    lax.fori_loop(0, blocks, back_attend, 0)

    def input_sums(here):
        tally(0, qkv[here, 0:width].astype(f32))
        tally(1, qkv[here, 2 * width : 3 * width].astype(f32))

    row_pass(64, input_sums)

    def back_qkv(t, span):
        back_low[:, span] = (mm_nt(qkv[...], w_qkv[span, :]) + grad_wide[:, span]).astype(bf16)

    tiles(width, back_qkv)
    grad_gather = CtxGather(links, back_low, all_grad, ctx, wsh, ctxs, 2)
    turned[...] = inputs[...].T

    def qkv_grad(t, span):
        w_qkv[:, span] = mm(turned[...], qkv[:, span]).astype(bf16)

    tiles(3 * width, qkv_grad)
    scatters[0].send_core()
    grad_gather.advance()
    table = TableSum(links, small, small_slots, place, zs, ctxs)
    table_steps = table.steps()
    next(table_steps)
    qkv_steps = scatters[0].steps()
    next(qkv_steps)
    next(table_steps)
    next(up_steps)
    next(down_steps)
    next(out_steps)
    bring_home(out_gather, result_low, home_out)
    while grad_gather.step < grad_gather.steps:
        grad_gather.advance()
    running = [down_steps, up_steps, out_steps, qkv_steps, table_steps]
    while running:
        still = []
        for steps in running:
            if next(steps, "end") != "end":
                still.append(steps)
        running = still
    bring_home(grad_gather, back_low, home_grad)
    copies = []
    for scatter, result in zip(scatters, (sum_qkv, sum_out, sum_up, sum_down)):
        copies.append(links.local(scatter.whole.at[scatter.span(0, core)], result))
    sum_small[...] = small[...]
    links.drain()
    for copy in copies:
        copy.wait()


def on_device(
    ctxs,
    wshs,
    tokens,
    cluster_order,
    qkv_weight,
    query_bias,
    value_bias,
    out_weight,
    out_bias,
    first_gain,
    first_shift,
    up_weight,
    up_bias,
    down_weight,
    down_bias,
    second_gain,
    second_shift,
    cotangent,
):
    rows, width = tokens.shape[1:]
    wide = up_weight.shape[1]
    zs = wshs // 2
    length = query_bias.shape[0]
    order = cluster_order[0]
    order_column = jnp.broadcast_to(order[:, None], (rows, LANES))
    order_row = jnp.broadcast_to(order[None, :], (8, rows))
    vectors = jnp.concatenate(
        [
            jnp.stack(
                [
                    query_bias,
                    value_bias,
                    out_bias,
                    first_gain,
                    first_shift,
                    down_bias,
                    second_gain,
                    second_shift,
                ]
            ),
            up_bias.reshape(4, length),
        ],
        axis=0,
    )
    vectors = jnp.pad(vectors, ((0, 4), (0, LANES - length)))
    small_rows = 8 * (width // STEP) + wide // STEP
    small_rows = (small_rows + 7) // 8 * 8
    heads_pairs = width // LANES
    blocks = rows // CLUSTER
    hops = 1 + len(bits_of(zs)) + len(bits_of(ctxs))
    shards = [qkv_weight.shape, out_weight.shape, up_weight.shape, down_weight.shape]
    slots = zs - 1
    sems = 4 * 2 * ctxs * 2 + 6 * zs * 4 + 4 * (4 * zs + 8) + 64

    def vmem(shape, dtype=bf16):
        return pltpu.VMEM(shape, dtype)

    anywhere = pl.BlockSpec(memory_space=pl.ANY)
    on_chip = pl.BlockSpec(memory_space=pltpu.VMEM)
    many = jax.ShapeDtypeStruct((ctxs, rows, width), bf16)
    pairs = (1, 2, 1, 2)
    results = pl.pallas_call(
        functools.partial(layer_kernel, ctxs, zs, pairs),
        out_shape=[
            jax.ShapeDtypeStruct((rows, width), bf16),
            jax.ShapeDtypeStruct((rows, width), bf16),
        ]
        + [jax.ShapeDtypeStruct(s, bf16) for s in shards]
        + [jax.ShapeDtypeStruct((small_rows, STEP), f32)]
        + [many] * 4,
        in_specs=[anywhere, anywhere, on_chip, on_chip] + [anywhere] * 5,
        out_specs=[on_chip, on_chip] + [anywhere] * 4 + [on_chip] + [anywhere] * 4,
        scratch_shapes=[
            vmem((ctxs, 8, rows), jnp.int32),
            vmem((wshs, 16, LANES)),
            vmem((width, 3 * width)),
            vmem((width, width)),
            vmem((width, wide)),
            vmem((wide, width)),
            vmem((wide, width)),
            vmem((2, rows, width)),
            vmem((rows, width), f32),
            vmem((rows, width)),
            vmem((rows, width)),
            vmem((rows, width)),
            vmem((rows, 3 * width)),
            vmem((blocks * heads_pairs, 2 * CLUSTER, CLUSTER), f32),
            vmem((rows, width)),
            vmem((width, rows)),
            vmem((rows, width), f32),
            vmem((rows, 1), f32),
            vmem((rows, wide)),
            vmem((rows, wide)),
            vmem((rows, width), f32),
            vmem((rows, width)),
            vmem((rows, width)),
            vmem((rows, width)),
            vmem((8, width), f32),
            vmem((8, wide), f32),
            vmem((small_rows, STEP), f32),
            vmem((hops, small_rows, STEP), f32),
        ]
        + [vmem((zs,) + s) for s in shards]
        + [vmem((slots,) + s) for s in shards]
        + [vmem((len(bits_of(ctxs)),) + s) for s in shards]
        + [pltpu.SemaphoreType.DMA((sems,)), pltpu.SemaphoreType.DMA((sems,))],
        compiler_params=pltpu.CompilerParams(
            collective_id=0, has_side_effects=True, vmem_limit_bytes=67043328
        ),
        name="layer",
    )(
        tokens[0],
        cotangent[0],
        order_column,
        order_row,
        vectors,
        qkv_weight,
        out_weight,
        up_weight,
        down_weight,
    )
    home_out, home_grad, sum_qkv, sum_out, sum_up, sum_down, small = results[:7]
    count = width // STEP
    whole = [small[n * count : (n + 1) * count].reshape(width) for n in range(8)]
    whole.append(small[8 * count : 8 * count + wide // STEP].reshape(wide))
    me = lax.axis_index("wsh")

    def own(vector):
        n = vector.shape[0] // wshs
        return lax.dynamic_slice_in_dim(vector, me * n, n, 0)

    (g_q, g_v, g_o, g_g1, g_s1, g_d, g_g2, g_s2, g_u) = [own(v) for v in whole]
    return (
        home_out[None],
        home_grad[None].astype(f32),
        sum_qkv.astype(f32),
        g_q,
        g_v,
        sum_out.astype(f32),
        g_o,
        g_g1,
        g_s1,
        sum_up.astype(f32),
        g_u,
        sum_down.astype(f32),
        g_d,
        g_g2,
        g_s2,
    )


def solution(mesh):
    row = P("wsh", None)
    vec = P("wsh")
    seq = P("wsh", "ctx", None)
    in_specs = (
        seq,
        P("wsh", "ctx"),
        row,
        vec,
        vec,
        row,
        vec,
        vec,
        vec,
        row,
        vec,
        row,
        vec,
        vec,
        vec,
        seq,
    )
    out_specs = (
        seq,
        seq,
        row,
        vec,
        vec,
        row,
        vec,
        vec,
        vec,
        row,
        vec,
        row,
        vec,
        vec,
        vec,
    )
    return jax.shard_map(
        functools.partial(on_device, mesh.shape["ctx"], mesh.shape["wsh"]),
        mesh=mesh,
        in_specs=in_specs,
        out_specs=out_specs,
        check_vma=False,
    )
```

time: 663 us -> 364 us (0.55); the launches traced: 654 us -> 363 us
  waiting for transfers between devices: 452 us -> 0 us
  Pallas kernels: 0 us -> 342 us
  matrix products: 82.2 us -> 0 us
  blocking collectives: 61.3 us -> 0 us
  between operations: 15.3 us -> 0.7 us
  other arithmetic: 20.3 us -> 7.47 us
  local copies, waits for them, and re-layouts: 22.8 us -> 12.9 us
    pallas_call x0 -> x1, Pallas kernels: none -> 342 us  [on_device(): pl.pallas_call(functools.partial(layer_kernel, ctxs, zs, pairs), out_shap...]
    all_gather x7 -> x0, waiting for transfers between devices: 234 us -> none  [the longest x1 53.9 us: on_device(): lax.all_gather(jnp.concatenate([tokens[0], cotangent[0]], axis=1), 'ctx',...]
    reduce_scatter x4 -> x0, waiting for transfers between devices: 151 us -> none  [summed(): part = lax.psum_scatter(grad, 'wsh', scatter_dimension=0, tiled=True)]
    dot_general x21 -> x0, matrix products: 82.2 us -> none  [the longest x4 19.6 us: inner(): lax.dot_general(left, right, (((0,), (0,)), ((), ())), preferred_element_...]
    psum x1 -> x0, waiting for transfers between devices: 63.9 us -> none  [summed(): return lax.psum(part, 'ctx').astype(jnp.float32)]
    psum x1 -> x0, blocking collectives: 37.6 us -> none  [on_device(): table = lax.psum(table, ('ctx', 'wsh'))]
    all_gather x2 -> x0, blocking collectives: 23.7 us -> none  [the longest x1 15.7 us: on_device(): packed = lax.all_gather(jnp.concatenate(small), 'wsh', axis=0, tiled=False)]
    convert_element_type x14 -> x0, local copies, waits for them, and re-layouts: 7.36 us -> none  [the longest x1 2.63 us: on_device(): grad_valued = jnp.einsum('chij,cihd->cjhd', probs, grad_context, preferre...]
  transfers between devices with their start and end apart: 12 -> 0, of which waited for: 10 -> 0; matrix products, arithmetic and copies ran while one was open for 11% -> 0% of each run, Pallas kernels for 0% -> 0%
where the time goes in v2:
time: 364 us; the launch traced here: 363 us
  Pallas kernels  342 us (94%)
  local copies, waits for them, and re-layouts  12.9 us (4%)
  other arithmetic  7.47 us (2%)
    pallas_call x1, Pallas kernels, on_device(): pl.pallas_call(functools.partial(layer_kernel, ctxs, zs, pairs), out_shap...  342 us

profile of v2, /device:TPU:0, one launch (start us, length us, event | category | flops | bytes accessed | tf_op | source)
XLA Modules:
  0.0 362.6 jit_solution(11648178271960411280)
XLA Ops:
  0.6 1.5 broadcast_in_dim.17.order_column
  2.2 1.3 broadcast_in_dim.18.order_row
  3.5 0.8 reshape.63
  4.2 0.8 concatenate.3
  5.0 0.6 pad.4.vectors
  5.6 341.6 %layer.1 = (bf16[512,768]{1,0:T(8,128)(2,1)}, bf16[512,768]{1,0:T(8,128)(2,1)}, bf16[96,2304]{1,0:T(8,128)(2,1)}, bf16[96,768]{1,0:T(8,128)(2,1)}, bf16[96,3072]...) custom-call(bf16[512,768]{1,0:T(8,128)(2,1)} %bitcast.16, ...), custom_call_target="tpu_custom_call" | custom-call | tf_op jit(solution)/shard_map/layer/pallas_call | solution.py:914
  347.2 0.0 copy-start.1
  347.2 0.0 copy-start.2
  347.3 0.9 fusion
  348.2 0.6 dynamic_slice.27
  348.8 0.6 dynamic_slice.28
  349.4 0.6 dynamic_slice.29
  349.9 0.6 dynamic_slice.30
  350.5 0.6 dynamic_slice.31
  351.1 0.6 dynamic_slice.33
  351.7 0.6 dynamic_slice.34
  352.3 0.6 dynamic_slice.35
  352.9 0.7 slice.32
  353.6 0.7 dynamic_slice.32
  354.3 0.0 copy-start.3
  354.3 2.4 bitcast_convert_fusion
  356.7 0.0 copy-start
  356.7 2.2 convert_element_type.24
  359.0 0.0 copy-done.1
  359.0 1.1 convert_element_type.25
  360.1 0.0 copy-done.2
  360.1 1.0 convert_element_type.22
  361.0 0.0 copy-done.3
  361.0 0.7 convert_element_type.23
  361.8 0.0 copy-done
  361.8 0.9 copy.32
  (9 shorter events, 0.1 us)
Async XLA Ops:
  347.2 11.7 %copy-start.1 = (bf16[384,768]{1,0:T(8,128)(2,1)S(1)}, bf16[384,768]{1,0:T(8,128)(2,1)}, u32[]{:S(2)}) copy-start(bf16[384,768]{1,0:T(8,128)(2,1)} %get-tuple-element.28) | copy-start | bytes 1769476
  347.2 12.8 %copy-start.2 = (bf16[96,2304]{1,0:T(8,128)(2,1)S(1)}, bf16[96,2304]{1,0:T(8,128)(2,1)}, u32[]{:S(2)}) copy-start(bf16[96,2304]{1,0:T(8,128)(2,1)} %get-tuple-element.24) | copy-start | bytes 1327108
  354.3 6.7 %copy-start.3 = (bf16[96,768]{1,0:T(8,128)(2,1)S(1)}, bf16[96,768]{1,0:T(8,128)(2,1)}, u32[]{:S(2)}) copy-start(bf16[96,768]{1,0:T(8,128)(2,1)} %get-tuple-element.26) | copy-start | bytes 442372
  356.7 5.1 %copy-start = (bf16[512,768]{1,0:T(8,128)(2,1)S(1)}, bf16[512,768]{1,0:T(8,128)(2,1)}, u32[]{:S(2)}) copy-start(bf16[512,768]{1,0:T(8,128)(2,1)} %get-tuple-element.22) | copy-start | bytes 2359300

commit v3 on v2

--- a/solution.py
+++ b/solution.py
@@ -51,17 +51,28 @@
     return value & -value
 
 
+def only_if(condition, action):
+    if condition is None:
+        action()
+    else:
+        pl.when(condition)(action)
+
+
 class Flight:
-    def __init__(self, copy):
-        self.copy, self.leaving = copy, True
-        copy.start()
+    def __init__(self, copy, landing=None, sends=None, receives=None):
+        self.copy, self.landing = copy, landing or copy
+        self.sends, self.receives = sends, receives
+        self.leaving = self.coming = True
+        only_if(sends, copy.start)
 
     def wait_recv(self):
-        self.copy.wait_recv()
+        if self.coming:
+            only_if(self.receives, self.landing.wait_recv)
+        self.coming = False
 
     def wait_send(self):
         if self.leaving:
-            self.copy.wait_send()
+            only_if(self.sends, self.copy.wait_send)
         self.leaving = False
 
 
@@ -70,19 +81,22 @@
         self.send_sem, self.recv_sem, self.used = send_sem, recv_sem, 0
         self.sent = []
 
-    def send(self, src, dst, ctx, wsh):
+    def remote(self, n, src, dst, ctx, wsh):
+        return pltpu.make_async_remote_copy(
+            src_ref=src,
+            dst_ref=dst,
+            send_sem=self.send_sem.at[n],
+            recv_sem=self.recv_sem.at[n],
+            device_id=(ctx, wsh),
+            device_id_type=pl.DeviceIdType.MESH,
+        )
+
+    def send(self, src, dst, ctx, wsh, landing=None, sends=None, receives=None):
         n = self.used
         self.used += 1
-        flight = Flight(
-            pltpu.make_async_remote_copy(
-                src_ref=src,
-                dst_ref=dst,
-                send_sem=self.send_sem.at[n],
-                recv_sem=self.recv_sem.at[n],
-                device_id=(ctx, wsh),
-                device_id_type=pl.DeviceIdType.MESH,
-            )
-        )
+        if landing is not None:
+            landing = self.remote(n, landing, landing, ctx, wsh)
+        flight = Flight(self.remote(n, src, dst, ctx, wsh), landing, sends, receives)
         self.sent.append(flight)
         return flight
 
@@ -94,8 +108,8 @@
         return copy
 
     def drain(self):
-        for copy in self.sent:
-            copy.wait_send()
+        for flight in self.sent:
+            flight.wait_send()
         self.sent = []
 
 
@@ -134,19 +148,17 @@
 
 
 class WeightGather:
-    def __init__(self, links, shard, whole, place, sizes, pair):
+    def __init__(self, links, shard, whole, place, zs, pair):
         self.links, self.shard, self.whole = links, shard, whole
         self.ctx, self.z, self.core = place
-        self.zs = sizes
-        self.pair = pair
+        self.zs, self.pair = zs, pair
         self.rows, self.columns = shard.shape
-        self.bits = bits_of(sizes)[::-1]
-
-    def row_span(self, offset, core):
-        first = (flip(self.z, offset) * 2 + core) * self.rows
-        return pl.ds(pl.multiple_of(first, 16), self.rows)
-
-    def column_span(self, mine):
+        self.moving, self.from_pair, self.from_core = {}, [], []
+
+    def row_span(self, z, core):
+        return pl.ds(pl.multiple_of((z * 2 + core) * self.rows, 16), self.rows)
+
+    def side(self, mine):
         if self.pair is None:
             return pl.ds(0, self.columns)
         half = self.columns // 2
@@ -155,173 +167,244 @@
             side = 1 - side
         return pl.ds(pl.multiple_of(side * half, LANES), half)
 
-    def wsh_of(self, offset, core):
-        return flip(self.z, offset) * 2 + core
+    def away(self, way, hop):
+        return (self.z - way * hop + 2 * self.zs) % self.zs
+
+    def arrives(self, way, hop):
+        return self.z >= hop if way > 0 else self.z + hop < self.zs
+
+    def can_send(self, way):
+        return self.z + 1 < self.zs if way > 0 else self.z > 0
+
+    def forward(self, way, hop, src):
+        mine = self.side(True)
+        here = self.away(way, hop)
+        sends = self.can_send(way)
+        if hop > 0:
+            sends = jnp.logical_and(sends, self.arrives(way, hop))
+        self.moving[way, hop + 1] = self.links.send(
+            src,
+            self.whole.at[self.row_span(here, self.core), mine],
+            self.ctx,
+            self.away(way, -1) * 2 + self.core,
+            landing=self.whole.at[self.row_span(self.away(way, hop + 1), self.core), mine],
+            sends=sends,
+            receives=self.arrives(way, hop + 1),
+        )
 
     def start(self):
-        span = self.column_span(True)
-        rows = self.row_span(0, self.core)
-        self.from_z, self.from_pair, self.from_core = {}, {}, []
-        for bit in self.bits:
-            self.from_z[bit] = self.links.send(
-                self.shard.at[:, span],
-                self.whole.at[rows, span],
-                self.ctx,
-                self.wsh_of(bit, self.core),
-            )
+        rows = self.row_span(self.z, self.core)
+        for way in (1, -1):
+            self.forward(way, 0, self.shard.at[:, self.side(True)])
         self.from_core.append(
             self.links.send(
-                self.shard, self.whole.at[rows], self.ctx, self.wsh_of(0, 1 - self.core)
+                self.shard, self.whole.at[rows], self.ctx, self.z * 2 + 1 - self.core
             )
         )
         self.own = self.links.local(self.shard, self.whole.at[rows])
 
-    def to_core(self, offset, span):
-        part = self.whole.at[self.row_span(offset, self.core), span]
+    def to_core(self, z, span, condition):
+        part = self.whole.at[self.row_span(z, self.core), span]
+        back = self.whole.at[self.row_span(z, 1 - self.core), span]
         self.from_core.append(
-            self.links.send(part, part, self.ctx, self.wsh_of(0, 1 - self.core))
+            self.links.send(
+                part,
+                part,
+                self.ctx,
+                self.z * 2 + 1 - self.core,
+                landing=back,
+                sends=condition,
+                receives=condition,
+            )
         )
 
-    def take_z(self):
-        span = self.column_span(True)
-        for offset in sorted(range(1, self.zs), key=lambda o: (-low_bit(o), o)):
-            self.from_z[offset].wait_recv()
-            part = self.whole.at[self.row_span(offset, self.core), span]
-            for bit in self.bits:
-                if bit < low_bit(offset):
-                    self.from_z[offset + bit] = self.links.send(
-                        part, part, self.ctx, self.wsh_of(bit, self.core)
-                    )
+    def hop(self, hop):
+        mine = self.side(True)
+        for way in (1, -1):
+            self.moving.pop((way, hop)).wait_recv()
+            z = self.away(way, hop)
+            part = self.whole.at[self.row_span(z, self.core), mine]
+            condition = self.arrives(way, hop)
+            if hop + 1 < self.zs:
+                self.forward(way, hop, part)
             if self.pair is not None:
-                self.from_pair[offset] = self.links.send(
-                    part, part, flip(self.ctx, self.pair), self.wsh_of(0, self.core)
+                flight = self.links.send(
+                    part,
+                    part,
+                    flip(self.ctx, self.pair),
+                    self.z * 2 + self.core,
+                    landing=self.whole.at[self.row_span(z, self.core), self.side(False)],
+                    sends=condition,
+                    receives=condition,
                 )
-            self.to_core(offset, span)
+                self.from_pair.append((z, condition, flight))
+            self.to_core(z, mine, condition)
 
     def take_pair(self):
-        if self.pair is None:
-            return
-        span = self.column_span(False)
-        for offset, arrival in self.from_pair.items():
-            arrival.wait_recv()
-            self.to_core(offset, span)
+        for z, condition, flight in self.from_pair:
+            flight.wait_recv()
+            self.to_core(z, self.side(False), condition)
+        self.from_pair = []
 
     def finish(self):
         self.own.wait()
-        for arrival in self.from_core:
-            arrival.wait_recv()
+        for flight in self.from_core:
+            flight.wait_recv()
 
 
 class GradScatter:
-    def __init__(self, links, whole, from_core, from_z, from_ctx, place, zs, ctxs):
-        self.links, self.whole = links, whole
-        self.from_core, self.from_z, self.from_ctx = from_core, from_z, from_ctx
+    def __init__(self, links, whole, final, buffers, place, zs, ctxs, pair):
+        self.links, self.whole, self.final = links, whole, final
+        self.from_core, self.from_pair, self.from_z, self.from_ctx, self.other = buffers
         self.ctx, self.z, self.core = place
-        self.zs, self.ctxs = zs, ctxs
-        self.rows = whole.shape[0] // (2 * zs)
-        self.zbits, self.cbits = bits_of(zs), bits_of(ctxs)
-        self.order = sorted(range(zs), key=lambda o: -(o % 2))
+        self.zs, self.pair = zs, pair
+        self.rows, self.columns = whole.shape[0] // (2 * zs), whole.shape[1]
+        self.cbits = [b for b in bits_of(ctxs) if b != pair]
+        self.order = list(range(1, zs)) + [0]
 
     def span(self, offset, core):
         first = (flip(self.z, offset) * 2 + core) * self.rows
         return pl.ds(pl.multiple_of(first, 16), self.rows)
 
+    def side(self, mine):
+        if self.pair is None:
+            return pl.ds(0, self.columns)
+        half = self.columns // 2
+        side = (self.ctx // self.pair) % 2
+        if not mine:
+            side = 1 - side
+        return pl.ds(pl.multiple_of(side * half, LANES), half)
+
+    def wsh_of(self, offset, core):
+        return flip(self.z, offset) * 2 + core
+
     def send_core(self):
-        self.arrive = {}
+        self.flights = []
         for offset in self.order:
-            self.arrive[offset] = self.links.send(
-                self.whole.at[self.span(offset, 1 - self.core)],
-                self.from_core.at[offset],
-                self.ctx,
-                self.z * 2 + 1 - self.core,
+            self.flights.append(
+                self.links.send(
+                    self.whole.at[self.span(offset, 1 - self.core)],
+                    self.from_core.at[offset],
+                    self.ctx,
+                    self.wsh_of(0, 1 - self.core),
+                )
             )
 
-    def add(self, offset, other):
+    def add(self, offset, columns, others):
         first = (flip(self.z, offset) * 2 + self.core) * self.rows
-        columns = self.whole.shape[1]
-        piece = 48 if columns <= 768 else 16
+        piece = 48
 
         def body(i, carry):
             here = pl.ds(pl.multiple_of(first + i * piece, 16), piece)
             there = pl.ds(pl.multiple_of(i * piece, 16), piece)
-            self.whole[here, :] = (
-                self.whole[here, :].astype(f32) + other[there, :].astype(f32)
-            ).astype(bf16)
+            total = self.whole[here, columns].astype(f32)
+            for other in others:
+                total = total + other[there, :].astype(f32)
+            self.whole[here, columns] = total.astype(bf16)
             return carry
 
         lax.fori_loop(0, self.rows // piece, body, 0)
 
-    def add_core(self):
-        for offset in self.order:
-            self.arrive[offset].wait_recv()
-            self.add(offset, self.from_core.at[offset])
-
-    def z_slot(self, bit, offset):
-        first = 0
-        for earlier in self.zbits:
-            if earlier == bit:
-                break
-            first += self.zs // (2 * earlier)
-        return first + offset // (2 * bit)
-
-    def send_z(self, bit):
-        self.arrive = {}
-        for offset in range(bit, self.zs, 2 * bit):
-            self.arrive[offset - bit] = self.links.send(
-                self.whole.at[self.span(offset, self.core)],
-                self.from_z.at[self.z_slot(bit, offset - bit)],
-                self.ctx,
-                flip(self.z, bit) * 2 + self.core,
+    def send_pair(self, offset):
+        columns = self.side(False)
+        return self.links.send(
+            self.whole.at[self.span(offset, self.core), columns],
+            self.from_pair.at[offset],
+            flip(self.ctx, self.pair),
+            self.wsh_of(0, self.core),
+        )
+
+    def send_z(self, offset):
+        columns = self.side(True)
+        return self.links.send(
+            self.whole.at[self.span(offset, self.core), columns],
+            self.from_z.at[offset - 1],
+            self.ctx,
+            self.wsh_of(offset, self.core),
+        )
+
+    def steps(self):
+        along_z = {}
+        in_pair = {}
+        for offset, flight in zip(self.order, self.flights):
+            flight.wait_recv()
+            self.add(offset, pl.ds(0, self.columns), [self.from_core.at[offset]])
+            if self.pair is not None:
+                in_pair[offset] = self.send_pair(offset)
+            elif offset > 0:
+                along_z[offset] = self.send_z(offset)
+        yield
+        mine = self.side(True)
+        for offset, flight in in_pair.items():
+            flight.wait_recv()
+            self.add(offset, mine, [self.from_pair.at[offset]])
+            if offset > 0:
+                along_z[offset] = self.send_z(offset)
+        if self.pair is not None:
+            yield
+        for flight in along_z.values():
+            flight.wait_recv()
+        self.add(0, mine, [self.from_z.at[offset - 1] for offset in along_z])
+        half = self.columns // 2
+        if self.pair is None:
+            parts = [(pl.ds(0, half), self.cbits), (pl.ds(half, half), self.cbits[::-1])]
+        else:
+            parts = [(mine, self.cbits)]
+        for step in range(len(self.cbits)):
+            flights = []
+            for columns, order in parts:
+                there = columns if self.pair is None else pl.ds(0, half)
+                flights.append(
+                    self.links.send(
+                        self.whole.at[self.span(0, self.core), columns],
+                        self.from_ctx.at[step, :, there],
+                        flip(self.ctx, order[step]),
+                        self.wsh_of(0, self.core),
+                    )
+                )
+            yield
+            for flight in flights:
+                flight.wait_recv()
+                flight.wait_send()
+            self.add(0, mine, [self.from_ctx.at[step]])
+        done = self.whole.at[self.span(0, self.core), mine]
+        self.results = [self.links.local(done, self.final.at[:, mine])]
+        if self.pair is not None:
+            flight = self.links.send(
+                done, self.other, flip(self.ctx, self.pair), self.wsh_of(0, self.core)
             )
-
-    def add_z(self, bit):
-        for offset, arrival in self.arrive.items():
-            arrival.wait_recv()
-            self.add(offset, self.from_z.at[self.z_slot(bit, offset)])
-
-    def send_ctx(self, bit):
-        self.arrive = self.links.send(
-            self.whole.at[self.span(0, self.core)],
-            self.from_ctx.at[self.cbits.index(bit)],
-            flip(self.ctx, bit),
-            self.z * 2 + self.core,
-        )
-
-    def add_ctx(self, bit):
-        self.arrive.wait_recv()
-        self.arrive.wait_send()
-        self.add(0, self.from_ctx.at[self.cbits.index(bit)])
-
-    def steps(self):
-        self.add_core()
-        for bit in self.zbits:
-            self.send_z(bit)
             yield
-            self.add_z(bit)
-        for bit in self.cbits:
-            self.send_ctx(bit)
-            yield
-            self.add_ctx(bit)
+            flight.wait_recv()
+            self.results.append(self.links.local(self.other, self.final.at[:, self.side(False)]))
         yield
 
 
 class TableSum:
     def __init__(self, links, table, slots, place, zs, ctxs):
         self.links, self.table, self.slots = links, table, slots
-        self.ctx, self.z, self.core = place
+        ctx, z, core = place
         self.hops = (
-            [(self.ctx, self.z * 2 + 1 - self.core)]
-            + [(self.ctx, flip(self.z, b) * 2 + self.core) for b in bits_of(zs)]
-            + [(flip(self.ctx, b), self.z * 2 + self.core) for b in bits_of(ctxs)]
+            [[(ctx, z * 2 + 1 - core)]]
+            + [[(ctx, flip(z, o) * 2 + core) for o in range(1, zs)]]
+            + [[(flip(ctx, b), z * 2 + core)] for b in bits_of(ctxs)]
         )
 
     def steps(self):
-        for n, (ctx, wsh) in enumerate(self.hops):
-            copy = self.links.send(self.table, self.slots.at[n], ctx, wsh)
+        slot = 0
+        for peers in self.hops:
+            flights = []
+            for n, peer in enumerate(peers):
+                flights.append(
+                    self.links.send(self.table, self.slots.at[slot + n], *peer)
+                )
             yield
-            copy.wait_recv()
-            copy.wait_send()
-            self.table[...] = self.table[...] + self.slots[n]
+            total = self.table[...]
+            for n, flight in enumerate(flights):
+                flight.wait_recv()
+                flight.wait_send()
+                total = total + self.slots[slot + n]
+            self.table[...] = total
+            slot += len(peers)
         yield
 
 
@@ -329,11 +412,20 @@
     ctxs,
     zs,
     pairs,
+    back_pairs,
     tok,
     cot,
-    order_column,
-    order_row,
-    vectors,
+    order,
+    order_block,
+    vec_0,
+    vec_1,
+    vec_2,
+    vec_3,
+    vec_4,
+    vec_5,
+    vec_6,
+    vec_7,
+    vec_8,
     qkv_shard,
     out_shard,
     up_shard,
@@ -344,11 +436,14 @@
     sum_out,
     sum_up,
     sum_down,
-    sum_small,
+    sum_768,
+    sum_wide,
     all_tok,
     all_cot,
     all_out,
     all_grad,
+    order_column,
+    vectors,
     all_order,
     all_vectors,
     w_qkv,
@@ -377,21 +472,11 @@
     row_up,
     small,
     small_slots,
-    core_qkv,
-    core_out,
-    core_up,
-    core_down,
-    z_qkv,
-    z_out,
-    z_up,
-    z_down,
-    c_qkv,
-    c_out,
-    c_up,
-    c_down,
-    send_sem,
-    recv_sem,
+    *rest,
 ):
+    buffers = [rest[5 * n : 5 * n + 5] for n in range(4)]
+    send_sem, recv_sem = rest[20:22]
+    vec_parts = rest[22:]
     rows, width = tok.shape
     wide = up_shard.shape[1]
     pairs_of_heads = width // LANES
@@ -403,64 +488,82 @@
     place = (ctx, z, core)
     links = Links(send_sem, recv_sem)
 
+    brought = [
+        links.local(vector, vec_parts[n])
+        for n, vector in enumerate(
+            (vec_0, vec_1, vec_2, vec_3, vec_4, vec_5, vec_6, vec_7, vec_8)
+        )
+    ]
+    vectors[...] = jnp.zeros_like(vectors)
+    for n, copy in enumerate(brought):
+        copy.wait()
+        vectors[n : n + 1, 0 : vec_parts[n].shape[0]] = vec_parts[n][...].reshape(1, -1)
+    order_column[...] = (
+        jnp.broadcast_to(order[...].astype(f32), (LANES, rows)).T.astype(jnp.int32)
+    )
+
     barrier = pltpu.get_barrier_semaphore()
-    peers = (
-        [(ctx, z * 2 + 1 - core)]
-        + [(ctx, flip(z, b) * 2 + core) for b in bits_of(zs)]
-        + [(flip(ctx, b), wsh) for b in bits_of(ctxs)]
-    )
+    stream_peers = [
+        (ctx, flip(z, o) * 2 + (core if same else 1 - core))
+        for o in range(zs)
+        for same in (True, False)
+        if o > 0 or not same
+    ]
+    peers = stream_peers + [(flip(ctx, b), wsh) for b in bits_of(ctxs)]
     for peer in peers:
         pl.semaphore_signal(barrier, 1, device_id=peer, device_id_type=pl.DeviceIdType.MESH)
     pl.semaphore_wait(barrier, len(peers))
 
     tok_gather = CtxGather(links, tok, all_tok, ctx, wsh, ctxs, 2)
     cot_gather = CtxGather(links, cot, all_cot, ctx, wsh, ctxs, 2)
-    order_gather = CtxGather(links, order_row, all_order, ctx, wsh, ctxs, 1)
-    tok_gather.advance()
-    order_gather.advance()
+    order_gather = CtxGather(links, order_block, all_order, ctx, wsh, ctxs, 1)
     vec_own = links.local(vectors, all_vectors.at[wsh])
-    vec_first = links.send(vectors, all_vectors.at[wsh], ctx, z * 2 + 1 - core)
-    gathers = [
+    vec_flights = [links.send(vectors, all_vectors.at[wsh], *peer) for peer in stream_peers]
+    q_gather, o_gather, u_gather, d_gather = [
         WeightGather(links, s, w, place, zs, p)
         for s, w, p in zip(
             (qkv_shard, out_shard, up_shard, down_shard), (w_qkv, w_out, w_up, w_down), pairs
         )
     ]
-    for gather in gathers:
-        gather.start()
-
-    vec_own.wait()
-    vec_first.wait_recv()
-    have = 2
-    for bit in bits_of(zs):
-        span = pl.ds((wsh // have) * have, have)
-        copy = links.send(all_vectors.at[span], all_vectors.at[span], ctx, flip(z, bit) * 2 + core)
-        copy.wait_recv()
-        have *= 2
+    tok_gather.advance()
+    order_gather.advance()
+    q_gather.start()
+    o_gather.start()
+    q_gather.hop(1)
+    o_gather.hop(1)
+    u_gather.start()
     while tok_gather.step < tok_gather.steps:
         tok_gather.advance()
         order_gather.advance()
+    for hop in range(2, zs):
+        q_gather.hop(hop)
+        o_gather.hop(hop)
+    cot_gather.advance()
+    vec_own.wait()
+    for flight in vec_flights:
+        flight.wait_recv()
 
     rows_768[...] = jnp.zeros_like(rows_768)
     row_up[...] = jnp.zeros_like(row_up)
     length = width // (2 * zs)
 
-    def spread(part, row, spot, target, target_row):
-        first = min(spot // LANES * LANES, target.shape[1] - STEP)
-        j = lax.broadcasted_iota(jnp.int32, (LANES, STEP), 0)
-        col = lax.broadcasted_iota(jnp.int32, (LANES, STEP), 1)
-        move = jnp.where((col == j + (spot - first)) & (j < length), 1.0, 0.0).astype(bf16)
-        moved = mm(part, move)
-        n = 8 if row is None else 1
-        at = 0 if row is None else row
-        where_to = pl.ds(target_row, n), pl.ds(first, STEP)
-        target[where_to] = target[where_to] + moved[at : at + n]
-
+    def spread(part, spot, size, target):
+        first = min(spot // LANES * LANES, target.shape[1] - 2 * part.shape[1])
+        shape = (part.shape[1], 2 * part.shape[1])
+        j = lax.broadcasted_iota(jnp.int32, shape, 0)
+        col = lax.broadcasted_iota(jnp.int32, shape, 1)
+        move = jnp.where((col == j + (spot - first)) & (j < size), 1.0, 0.0).astype(bf16)
+        at = pl.ds(first, shape[1])
+        target[:, at] = target[:, at] + mm(part, move)[: target.shape[0]]
+
+    length_up = wide // (2 * zs)
     for s in range(2 * zs):
-        part = all_vectors[s]
-        spread(part, None, length * s, rows_768, 0)
-        for r in range(4):
-            spread(part, 8 + r, length * (4 * s + r), row_up, 0)
+        spread(all_vectors[s, :, 0:LANES], length * s, length, rows_768)
+        if length_up % LANES == 0:
+            up_part = all_vectors[s, 8:16, 0:length_up].astype(f32)
+            row_up[0:1, length_up * s : length_up * (s + 1)] = up_part[0:1]
+        else:
+            spread(all_vectors[s, 8:16, :], length_up * s, length_up, row_up)
 
     def pick(gather, own, total):
         copies = {}
@@ -514,7 +617,7 @@
             if offset + 1 < ctxs:
                 fetch(offset + 1)
             if offset == 0:
-                places = order_row[...]
+                places = order[...]
             else:
                 order_gather.need(offset)
                 places = all_order[flip(ctx, offset)]
@@ -536,12 +639,12 @@
 
             lax.fori_loop(0, blocks, body, 0)
 
-    def tiles(columns, body):
+    def tiles(columns, body, first=0):
         def step(t, carry):
             body(t, pl.ds(pl.multiple_of(t * STEP, STEP), STEP))
             return carry
 
-        lax.fori_loop(0, columns // STEP, step, 0)
+        lax.fori_loop(first // STEP, columns // STEP, step, 0)
 
     def row_pass(size, body):
         def step(i, carry):
@@ -561,18 +664,18 @@
         rows_768.at[pl.ds(n, 1)] for n in range(8)
     ]
 
-    gathers[0].take_z()
+    u_gather.hop(1)
+    d_gather.start()
     pick(tok_gather, tok, acc)
 
     def keep_inputs(here):
         inputs[here, :] = acc[here, :].astype(bf16)
 
     row_pass(CLUSTER, keep_inputs)
-    gathers[1].take_z()
-    gathers[0].take_pair()
-    gathers[1].take_pair()
-    cot_gather.advance()
-    gathers[0].finish()
+    u_gather.hop(2)
+    q_gather.take_pair()
+    o_gather.take_pair()
+    q_gather.finish()
 
     def project(t, span):
         at = pl.ds(pl.multiple_of((t % (width // STEP)) * STEP, STEP), STEP)
@@ -582,7 +685,8 @@
 
     tiles(3 * width, project)
 
-    gathers[2].take_z()
+    d_gather.hop(1)
+    cot_gather.advance()
 
     lane = lax.broadcasted_iota(jnp.int32, (1, LANES), 1)
     left = jnp.where(lane < HEAD_DIM, 1.0, 0.0).astype(bf16)
@@ -599,7 +703,7 @@
 
     def attend(b, carry):
         here = pl.ds(pl.multiple_of(b * CLUSTER, CLUSTER), CLUSTER)
-        visible = order_row[0:1, here] <= order_column[here, :]
+        visible = order[0:1, here] <= order_column[here, :]
         hide = jnp.where(visible, 0.0, -1e30)
         hide = jnp.concatenate([hide, hide], axis=0)
         for pair in range(pairs_of_heads):
@@ -613,11 +717,9 @@
         return carry
 
     lax.fori_loop(0, blocks, attend, 0)
-    gathers[2].take_pair()
-    gathers[3].take_z()
-    while cot_gather.step < cot_gather.steps:
-        cot_gather.advance()
-    gathers[1].finish()
+    for hop in range(3, zs):
+        u_gather.hop(hop)
+    o_gather.finish()
 
     def out_project(t, span):
         acc[:, span] = mm(context[...], w_out[:, span])
@@ -635,14 +737,10 @@
         low[here, :] = (normed * gain1[...] + shift1[...]).astype(bf16)
 
     row_pass(64, first_normalize)
-    pick(cot_gather, cot, acc)
-
-    def keep_top(here):
-        top[here, :] = acc[here, :].astype(bf16)
-
-    row_pass(CLUSTER, keep_top)
-    gathers[3].take_pair()
-    gathers[2].finish()
+    u_gather.take_pair()
+    while cot_gather.step < cot_gather.steps:
+        cot_gather.advance()
+    u_gather.finish()
 
     def feed(t, span):
         pre = mm(low[...], w_up[:, span]) + row_up[0:1, span]
@@ -651,7 +749,17 @@
         slope[:, span] = (half + pre * jnp.exp(-0.5 * pre * pre) * 0.3989422804014327).astype(bf16)
 
     tiles(wide, feed)
-    gathers[3].finish()
+    d_gather.hop(2)
+    pick(cot_gather, cot, acc)
+
+    def keep_top(here):
+        top[here, :] = acc[here, :].astype(bf16)
+
+    row_pass(CLUSTER, keep_top)
+    for hop in range(3, zs):
+        d_gather.hop(hop)
+    d_gather.take_pair()
+    d_gather.finish()
 
     def down(t, span):
         acc[:, span] = mm(hidden[...], w_down[:, span])
@@ -682,15 +790,17 @@
     row_pass(64, second_normalize)
 
     scatters = [
-        GradScatter(links, w, a, b, c, place, zs, ctxs)
-        for w, a, b, c in (
-            (w_qkv, core_qkv, z_qkv, c_qkv),
-            (w_out, core_out, z_out, c_out),
-            (w_up, core_up, z_up, c_up),
-            (g_down, core_down, z_down, c_down),
+        GradScatter(links, w, f, b, place, zs, ctxs, p)
+        for w, f, b, p in zip(
+            (w_qkv, w_out, w_up, g_down),
+            (sum_qkv, sum_out, sum_up, sum_down),
+            buffers,
+            back_pairs,
         )
     ]
+    gathered, links.sent = links.sent, []
     out_gather = CtxGather(links, result_low, all_out, ctx, wsh, ctxs, 2)
+    out_gather.advance()
     part_rows = wide // (2 * zs)
 
     def down_grad(owner):
@@ -717,7 +827,6 @@
 
         tiles(wide, all_down)
         scatters[3].send_core()
-    out_gather.advance()
 
     def back_hidden(t, span):
         grad = (mm_nt(grad_low[...], w_down[span, :]) * slope[:, span]).astype(bf16)
@@ -726,9 +835,10 @@
             grad.astype(f32), axis=0, keepdims=True
         )
 
-    tiles(wide, back_hidden)
+    tiles(wide // 2, back_hidden)
     down_steps = scatters[3].steps()
     next(down_steps)
+    tiles(wide, back_hidden, wide // 2)
 
     def back_up(t, span):
         acc[:, span] = mm_nt(slope[...], w_up[span, :])
@@ -754,7 +864,8 @@
     row_pass(64, first_back)
     while out_gather.step < out_gather.steps:
         out_gather.advance()
-    links.drain()
+    for flight in gathered:
+        flight.wait_send()
 
     turned[...] = low[...].T
 
@@ -778,7 +889,6 @@
     scatters[1].send_core()
     up_steps = scatters[2].steps()
     next(up_steps)
-    next(down_steps)
     out_steps = scatters[1].steps()
     next(out_steps)
 
@@ -819,33 +929,67 @@
 
     tiles(3 * width, qkv_grad)
     scatters[0].send_core()
-    grad_gather.advance()
     table = TableSum(links, small, small_slots, place, zs, ctxs)
     table_steps = table.steps()
     next(table_steps)
+    next(out_steps)
+    bring_home(out_gather, result_low, home_out)
     qkv_steps = scatters[0].steps()
     next(qkv_steps)
+    grad_gather.advance()
     next(table_steps)
     next(up_steps)
+    while grad_gather.step < grad_gather.steps:
+        grad_gather.advance()
+    next(down_steps)
+    next(qkv_steps)
     next(down_steps)
     next(out_steps)
-    bring_home(out_gather, result_low, home_out)
-    while grad_gather.step < grad_gather.steps:
-        grad_gather.advance()
-    running = [down_steps, up_steps, out_steps, qkv_steps, table_steps]
+    next(table_steps)
+    next(down_steps)
+    next(out_steps)
+    next(up_steps)
+    bring_home(grad_gather, back_low, home_grad)
+    running = [down_steps, out_steps, up_steps, table_steps, qkv_steps]
     while running:
         still = []
         for steps in running:
             if next(steps, "end") != "end":
                 still.append(steps)
         running = still
-    bring_home(grad_gather, back_low, home_grad)
-    copies = []
-    for scatter, result in zip(scatters, (sum_qkv, sum_out, sum_up, sum_down)):
-        copies.append(links.local(scatter.whole.at[scatter.span(0, core)], result))
-    sum_small[...] = small[...]
+    count = width // STEP
+    for n in range(8):
+        for t in range(count):
+            sum_768[n : n + 1, t * STEP : (t + 1) * STEP] = small[n * count + t : n * count + t + 1]
+    for t in range(wide // STEP):
+        sum_wide[0:1, t * STEP : (t + 1) * STEP] = small[8 * count + t : 8 * count + t + 1]
     links.drain()
-    for copy in copies:
+    for scatter in scatters:
+        for result in scatter.results:
+            result.wait()
+
+
+def finish_kernel(wshs, *refs):
+    sources, (sum_768, sum_wide) = refs[:6], refs[6:8]
+    targets, vecs = refs[8:14], refs[14:23]
+    taken, given, sem = refs[23:29], refs[29:35], refs[35]
+    coming = [pltpu.make_async_copy(s, t, sem.at[n]) for n, (s, t) in enumerate(zip(sources, taken))]
+    for copy in coming:
+        copy.start()
+    me = lax.axis_index("wsh")
+    for sums, outs in ((sum_768, vecs[:8]), (sum_wide, vecs[8:])):
+        size = outs[0].shape[0]
+        columns = sums.shape[1]
+        mine = pltpu.roll(sums[...], lax.rem(columns - me * size, columns), 1)
+        for n, out in enumerate(outs):
+            out[...] = mine[n, 0:size]
+    going = []
+    for n, copy in enumerate(coming):
+        copy.wait()
+        given[n][...] = taken[n][...].astype(given[n].dtype)
+        going.append(pltpu.make_async_copy(given[n], targets[n], sem.at[6 + n]))
+        going[-1].start()
+    for copy in going:
         copy.wait()
 
 
@@ -872,59 +1016,53 @@
     rows, width = tokens.shape[1:]
     wide = up_weight.shape[1]
     zs = wshs // 2
-    length = query_bias.shape[0]
-    order = cluster_order[0]
-    order_column = jnp.broadcast_to(order[:, None], (rows, LANES))
-    order_row = jnp.broadcast_to(order[None, :], (8, rows))
-    vectors = jnp.concatenate(
-        [
-            jnp.stack(
-                [
-                    query_bias,
-                    value_bias,
-                    out_bias,
-                    first_gain,
-                    first_shift,
-                    down_bias,
-                    second_gain,
-                    second_shift,
-                ]
-            ),
-            up_bias.reshape(4, length),
-        ],
-        axis=0,
-    )
-    vectors = jnp.pad(vectors, ((0, 4), (0, LANES - length)))
     small_rows = 8 * (width // STEP) + wide // STEP
     small_rows = (small_rows + 7) // 8 * 8
+    vector_lanes = (up_bias.shape[0] + LANES - 1) // LANES * LANES
     heads_pairs = width // LANES
     blocks = rows // CLUSTER
-    hops = 1 + len(bits_of(zs)) + len(bits_of(ctxs))
+    hops = zs + len(bits_of(ctxs))
     shards = [qkv_weight.shape, out_weight.shape, up_weight.shape, down_weight.shape]
-    slots = zs - 1
-    sems = 4 * 2 * ctxs * 2 + 6 * zs * 4 + 4 * (4 * zs + 8) + 64
+    sems = 2 * wshs + 4 * 2 * ctxs * 2 + 10 * zs * 4 + 4 * (4 * zs + 8) + 64
 
     def vmem(shape, dtype=bf16):
         return pltpu.VMEM(shape, dtype)
 
+    pairs = (1, 1, 2, None)
+    back_pairs = (2, 2, 1, None)
+    landing = []
+    for (n, columns), pair in zip(shards, back_pairs):
+        part = columns // 2
+        landing.append(vmem((zs, n, columns)))
+        if pair is None:
+            landing.append(vmem((1, 16, LANES)))
+            landing.append(vmem((zs - 1, n, columns)))
+            landing.append(vmem((len(bits_of(ctxs)), n, columns)))
+            landing.append(vmem((16, LANES)))
+        else:
+            landing.append(vmem((zs, n, part)))
+            landing.append(vmem((zs - 1, n, part)))
+            landing.append(vmem((len(bits_of(ctxs)) - 1, n, part)))
+            landing.append(vmem((n, part)))
     anywhere = pl.BlockSpec(memory_space=pl.ANY)
     on_chip = pl.BlockSpec(memory_space=pltpu.VMEM)
     many = jax.ShapeDtypeStruct((ctxs, rows, width), bf16)
-    pairs = (1, 2, 1, 2)
     results = pl.pallas_call(
-        functools.partial(layer_kernel, ctxs, zs, pairs),
+        functools.partial(layer_kernel, ctxs, zs, pairs, back_pairs),
         out_shape=[
             jax.ShapeDtypeStruct((rows, width), bf16),
             jax.ShapeDtypeStruct((rows, width), bf16),
         ]
         + [jax.ShapeDtypeStruct(s, bf16) for s in shards]
-        + [jax.ShapeDtypeStruct((small_rows, STEP), f32)]
+        + [jax.ShapeDtypeStruct((8, width), f32), jax.ShapeDtypeStruct((8, wide), f32)]
         + [many] * 4,
-        in_specs=[anywhere, anywhere, on_chip, on_chip] + [anywhere] * 5,
-        out_specs=[on_chip, on_chip] + [anywhere] * 4 + [on_chip] + [anywhere] * 4,
+        in_specs=[anywhere, anywhere, on_chip, anywhere] + [anywhere] * 13,
+        out_specs=[on_chip, on_chip] + [anywhere] * 4 + [on_chip] * 2 + [anywhere] * 4,
         scratch_shapes=[
-            vmem((ctxs, 8, rows), jnp.int32),
-            vmem((wshs, 16, LANES)),
+            vmem((rows, LANES), jnp.int32),
+            vmem((16, vector_lanes)),
+            vmem((ctxs, 1, rows), jnp.int32),
+            vmem((wshs, 16, vector_lanes)),
             vmem((width, 3 * width)),
             vmem((width, width)),
             vmem((width, wide)),
@@ -952,10 +1090,10 @@
             vmem((small_rows, STEP), f32),
             vmem((hops, small_rows, STEP), f32),
         ]
-        + [vmem((zs,) + s) for s in shards]
-        + [vmem((slots,) + s) for s in shards]
-        + [vmem((len(bits_of(ctxs)),) + s) for s in shards]
-        + [pltpu.SemaphoreType.DMA((sems,)), pltpu.SemaphoreType.DMA((sems,))],
+        + landing
+        + [pltpu.SemaphoreType.DMA((sems,)), pltpu.SemaphoreType.DMA((sems,))]
+        + [vmem(query_bias.shape)] * 8
+        + [vmem(up_bias.shape)],
         compiler_params=pltpu.CompilerParams(
             collective_id=0, has_side_effects=True, vmem_limit_bytes=67043328
         ),
@@ -963,38 +1101,53 @@
     )(
         tokens[0],
         cotangent[0],
-        order_column,
-        order_row,
-        vectors,
+        cluster_order,
+        cluster_order,
+        query_bias,
+        value_bias,
+        out_bias,
+        first_gain,
+        first_shift,
+        down_bias,
+        second_gain,
+        second_shift,
+        up_bias,
         qkv_weight,
         out_weight,
         up_weight,
         down_weight,
     )
-    home_out, home_grad, sum_qkv, sum_out, sum_up, sum_down, small = results[:7]
-    count = width // STEP
-    whole = [small[n * count : (n + 1) * count].reshape(width) for n in range(8)]
-    whole.append(small[8 * count : 8 * count + wide // STEP].reshape(wide))
-    me = lax.axis_index("wsh")
-
-    def own(vector):
-        n = vector.shape[0] // wshs
-        return lax.dynamic_slice_in_dim(vector, me * n, n, 0)
-
-    (g_q, g_v, g_o, g_g1, g_s1, g_d, g_g2, g_s2, g_u) = [own(v) for v in whole]
+    big = results[:6]
+    part = width // wshs
+    part_wide = wide // wshs
+    outs = [jax.ShapeDtypeStruct((rows, width), bf16), jax.ShapeDtypeStruct((rows, width), f32)]
+    outs += [jax.ShapeDtypeStruct(s, f32) for s in shards]
+    outs += [jax.ShapeDtypeStruct((part,), f32)] * 8 + [jax.ShapeDtypeStruct((part_wide,), f32)]
+    (home_out, home_grad, g_qkv, g_out, g_up, g_down, *vecs) = pl.pallas_call(
+        functools.partial(finish_kernel, wshs),
+        out_shape=outs,
+        in_specs=[anywhere] * 6 + [on_chip] * 2,
+        out_specs=[anywhere] * 6 + [on_chip] * 9,
+        scratch_shapes=[vmem(v.shape) for v in big]
+        + [vmem(v.shape, o.dtype) for v, o in zip(big, outs)]
+        + [pltpu.SemaphoreType.DMA((12,))],
+        compiler_params=pltpu.CompilerParams(vmem_limit_bytes=67043328),
+        name="finish",
+    )(*big, *results[6:8])
+    g_q, g_v, g_o, g_g1, g_s1, g_d, g_g2, g_s2, g_u = vecs
     return (
         home_out[None],
-        home_grad[None].astype(f32),
-        sum_qkv.astype(f32),
+        home_grad[None],
+        g_qkv,
         g_q,
         g_v,
-        sum_out.astype(f32),
+        g_out,
         g_o,
         g_g1,
         g_s1,
-        sum_up.astype(f32),
+        g_up,
         g_u,
-        sum_down.astype(f32),
+        g_down,
         g_d,
         g_g2,
         g_s2,

time: 364 us -> 248 us (0.68)
  Pallas kernels: 342 us -> 247 us
  local copies, waits for them, and re-layouts: 12.9 us -> 0 us
  other arithmetic: 7.47 us -> 0 us
    pallas_call x1 -> x2, Pallas kernels: 342 us -> 247 us  [the longest x1 241 us: on_device(): pl.pallas_call(functools.partial(layer_kernel, ctxs, zs, pairs, back_pair...]
    convert_element_type x5 -> x0, other arithmetic: 7.47 us -> none  [the longest x1 2.42 us: on_device(): home_grad[None].astype(f32)]
    dynamic_slice x9 -> x0, local copies, waits for them, and re-layouts: 5.33 us -> none  [own(): return lax.dynamic_slice_in_dim(vector, me * n, n, 0)]
where the time goes in v3:
time: 248 us; the launch traced here: 247 us
  Pallas kernels  247 us (100%)
    pallas_call x1, Pallas kernels, on_device(): pl.pallas_call(functools.partial(layer_kernel, ctxs, zs, pairs, back_pair...  241 us
    pallas_call x1, Pallas kernels, on_device(): pl.pallas_call(functools.partial(finish_kernel, wshs), out_shape=outs, in...  5.39 us

profile of v3, /device:TPU:0, one launch (start us, length us, event | category | flops | bytes accessed | tf_op | source)
XLA Modules:
  0.0 247.4 jit_solution(15888416703338489822)
XLA Ops:
  0.7 241.2 %layer.1 = (bf16[512,768]{1,0:T(8,128)(2,1)}, bf16[512,768]{1,0:T(8,128)(2,1)}, bf16[96,2304]{1,0:T(8,128)(2,1)}, bf16[96,768]{1,0:T(8,128)(2,1)}, bf16[96,3072]...) custom-call(bf16[512,768]{1,0:T(8,128)(2,1)} %bitcast.4, ...), custom_call_target="tpu_custom_call" | custom-call | tf_op jit(solution)/shard_map/layer/pallas_call | solution.py:1050
  241.9 5.4 %finish.1 = (bf16[512,768]{1,0:T(8,128)(2,1)}, f32[512,768]{1,0:T(8,128)}, f32[96,2304]{1,0:T(8,128)}, f32[96,768]{1,0:T(8,128)}, f32[96,3072]{1,0:T(8,128)}, /*...) custom-call(bf16[512,768]{1,0:T(8,128)(2,1)} %get-tuple-element.38.r, ...), custom_call_target="tpu_custom_call" | custom-call | tf_op jit(solution)/shard_map/finish/pallas_call | solution.py:1126

commit v4 on v3

--- a/solution.py
+++ b/solution.py
@@ -148,7 +148,7 @@
 
 
 class WeightGather:
-    def __init__(self, links, shard, whole, place, zs, pair):
+    def __init__(self, links, shard, whole, pair, place, zs):
         self.links, self.shard, self.whole = links, shard, whole
         self.ctx, self.z, self.core = place
         self.zs, self.pair = zs, pair
@@ -260,7 +260,7 @@
         self.zs, self.pair = zs, pair
         self.rows, self.columns = whole.shape[0] // (2 * zs), whole.shape[1]
         self.cbits = [b for b in bits_of(ctxs) if b != pair]
-        self.order = list(range(1, zs)) + [0]
+        self.order = sorted(range(zs), key=lambda o: (-(o % 2), -o))
 
     def span(self, offset, core):
         first = (flip(self.z, offset) * 2 + core) * self.rows
@@ -318,33 +318,51 @@
         columns = self.side(True)
         return self.links.send(
             self.whole.at[self.span(offset, self.core), columns],
-            self.from_z.at[offset - 1],
+            self.from_z.at[self.slot(low_bit(offset), offset - low_bit(offset))],
             self.ctx,
-            self.wsh_of(offset, self.core),
+            self.wsh_of(low_bit(offset), self.core),
         )
 
+    def slot(self, bit, offset):
+        first = 0
+        for earlier in bits_of(bit):
+            first += self.zs // (2 * earlier)
+        return first + offset // (2 * bit)
+
     def steps(self):
-        along_z = {}
+        mine = self.side(True)
+        coming = {}
         in_pair = {}
+
+        def pass_on(offset):
+            if offset > 0:
+                coming[offset - low_bit(offset)] = self.send_z(offset)
+
         for offset, flight in zip(self.order, self.flights):
             flight.wait_recv()
             self.add(offset, pl.ds(0, self.columns), [self.from_core.at[offset]])
             if self.pair is not None:
                 in_pair[offset] = self.send_pair(offset)
-            elif offset > 0:
-                along_z[offset] = self.send_z(offset)
+            elif offset % 2:
+                pass_on(offset)
         yield
-        mine = self.side(True)
         for offset, flight in in_pair.items():
             flight.wait_recv()
             self.add(offset, mine, [self.from_pair.at[offset]])
-            if offset > 0:
-                along_z[offset] = self.send_z(offset)
-        if self.pair is not None:
+            if offset % 2:
+                pass_on(offset)
             yield
-        for flight in along_z.values():
-            flight.wait_recv()
-        self.add(0, mine, [self.from_z.at[offset - 1] for offset in along_z])
+        for bit in bits_of(self.zs):
+            taken, coming = coming, {}
+            for offset in sorted(taken, key=lambda o: -(o % (2 * bit) + (o & (2 * bit)))):
+                taken[offset].wait_recv()
+                self.add(offset, mine, [self.from_z.at[self.slot(bit, offset)]])
+                if offset & (2 * bit):
+                    pass_on(offset)
+                if offset:
+                    yield
+            if 2 * bit < self.zs:
+                yield
         half = self.columns // 2
         if self.pair is None:
             parts = [(pl.ds(0, half), self.cbits), (pl.ds(half, half), self.cbits[::-1])]
@@ -406,6 +424,38 @@
             self.table[...] = total
             slot += len(peers)
         yield
+
+
+DOWN_SPLIT = 256
+BACK_SPLIT = 512
+PAIRS = (1, 2, 2, 1)
+BACK_PAIRS = (1, 2, 2, None, 1)
+PLAN = (
+    ("t", "q0", "o0", "u0", "tx", "q1", "u1", "q2", "o1", "o2", "q3",),
+    ("u2", "e0", "d0", "r", "o3",),
+    ("u3", "c", "qp", "e1", "op", "qf",),
+    ("of",),
+    ("e2", "d1", "e3", "cx",),
+    ("up", "ep", "d2", "uf",),
+    ("d3", "P", "df", "rx", "ef",),
+)
+BACK = (
+    ("l",),
+    (),
+    ("d", "e", "l",),
+    (),
+    (),
+    ("e", "d",),
+    (),
+    ("u",),
+    ("e",),
+    (),
+    (
+        "e", "s", "u", "q", "q", "e", "d", "e", "o", "u", "e", "H", "g", "o", "o", "s", "u",
+        "d", "q", "u", "q", "o", "u", "e", "u", "q", "g", "q", "e", "u", "o", "o", "o", "q",
+        "s", "d", "q", "o", "s", "u", "q", "K", "o", "u", "e", "d", "s", "q", "o",
+    ),
+)
 
 
 def layer_kernel(
@@ -474,9 +524,10 @@
     small_slots,
     *rest,
 ):
-    buffers = [rest[5 * n : 5 * n + 5] for n in range(4)]
-    send_sem, recv_sem = rest[20:22]
-    vec_parts = rest[22:]
+    buffers = [rest[5 * n : 5 * n + 5] for n in range(5)]
+    send_sem, recv_sem = rest[25:27]
+    vec_parts = rest[27:]
+    back_split = BACK_SPLIT
     rows, width = tok.shape
     wide = up_shard.shape[1]
     pairs_of_heads = width // LANES
@@ -519,26 +570,50 @@
     order_gather = CtxGather(links, order_block, all_order, ctx, wsh, ctxs, 1)
     vec_own = links.local(vectors, all_vectors.at[wsh])
     vec_flights = [links.send(vectors, all_vectors.at[wsh], *peer) for peer in stream_peers]
-    q_gather, o_gather, u_gather, d_gather = [
-        WeightGather(links, s, w, place, zs, p)
-        for s, w, p in zip(
-            (qkv_shard, out_shard, up_shard, down_shard), (w_qkv, w_out, w_up, w_down), pairs
-        )
+    split = DOWN_SPLIT
+    parts = [
+        (qkv_shard, w_qkv, pairs[0]),
+        (out_shard, w_out, pairs[1]),
+        (up_shard, w_up, pairs[2]),
+        (down_shard.at[:, pl.ds(0, split)], w_down.at[:, pl.ds(0, split)], pairs[3]),
+        (
+            down_shard.at[:, pl.ds(split, width - split)],
+            w_down.at[:, pl.ds(split, width - split)],
+            None,
+        ),
     ]
-    tok_gather.advance()
-    order_gather.advance()
-    q_gather.start()
-    o_gather.start()
-    q_gather.hop(1)
-    o_gather.hop(1)
-    u_gather.start()
-    while tok_gather.step < tok_gather.steps:
-        tok_gather.advance()
-        order_gather.advance()
-    for hop in range(2, zs):
-        q_gather.hop(hop)
-        o_gather.hop(hop)
-    cot_gather.advance()
+    weights = dict(
+        zip("quoed", [WeightGather(links, *parts[n], place, zs) for n in (0, 2, 1, 3, 4)])
+    )
+    rows_in = {"t": tok_gather, "r": order_gather, "c": cot_gather}
+
+    def act(plan):
+        for step in plan:
+            if step == "P":
+                pick(cot_gather, cot, acc)
+                row_pass(CLUSTER, keep_top)
+                continue
+            if step[0] in rows_in:
+                gather = rows_in[step[0]]
+                if gather.step < gather.steps:
+                    gather.advance()
+                while step[1:] == "x" and gather.step < gather.steps:
+                    gather.advance()
+                continue
+            gather, kind = weights[step[0]], step[1]
+            if kind == "0":
+                gather.start()
+            elif kind == "3":
+                for hop in range(3, zs):
+                    gather.hop(hop)
+            elif kind in "12":
+                gather.hop(int(kind))
+            elif kind == "p":
+                gather.take_pair()
+            else:
+                gather.finish()
+
+    act(PLAN[0])
     vec_own.wait()
     for flight in vec_flights:
         flight.wait_recv()
@@ -564,6 +639,9 @@
             row_up[0:1, length_up * s : length_up * (s + 1)] = up_part[0:1]
         else:
             spread(all_vectors[s, 8:16, :], length_up * s, length_up, row_up)
+
+    def keep_top(here):
+        top[here, :] = acc[here, :].astype(bf16)
 
     def pick(gather, own, total):
         copies = {}
@@ -664,18 +742,14 @@
         rows_768.at[pl.ds(n, 1)] for n in range(8)
     ]
 
-    u_gather.hop(1)
-    d_gather.start()
+    act(PLAN[1])
     pick(tok_gather, tok, acc)
 
     def keep_inputs(here):
         inputs[here, :] = acc[here, :].astype(bf16)
 
     row_pass(CLUSTER, keep_inputs)
-    u_gather.hop(2)
-    q_gather.take_pair()
-    o_gather.take_pair()
-    q_gather.finish()
+    act(PLAN[2])
 
     def project(t, span):
         at = pl.ds(pl.multiple_of((t % (width // STEP)) * STEP, STEP), STEP)
@@ -685,8 +759,7 @@
 
     tiles(3 * width, project)
 
-    d_gather.hop(1)
-    cot_gather.advance()
+    act(PLAN[3])
 
     lane = lax.broadcasted_iota(jnp.int32, (1, LANES), 1)
     left = jnp.where(lane < HEAD_DIM, 1.0, 0.0).astype(bf16)
@@ -717,9 +790,7 @@
         return carry
 
     lax.fori_loop(0, blocks, attend, 0)
-    for hop in range(3, zs):
-        u_gather.hop(hop)
-    o_gather.finish()
+    act(PLAN[4])
 
     def out_project(t, span):
         acc[:, span] = mm(context[...], w_out[:, span])
@@ -737,10 +808,7 @@
         low[here, :] = (normed * gain1[...] + shift1[...]).astype(bf16)
 
     row_pass(64, first_normalize)
-    u_gather.take_pair()
-    while cot_gather.step < cot_gather.steps:
-        cot_gather.advance()
-    u_gather.finish()
+    act(PLAN[5])
 
     def feed(t, span):
         pre = mm(low[...], w_up[:, span]) + row_up[0:1, span]
@@ -749,17 +817,7 @@
         slope[:, span] = (half + pre * jnp.exp(-0.5 * pre * pre) * 0.3989422804014327).astype(bf16)
 
     tiles(wide, feed)
-    d_gather.hop(2)
-    pick(cot_gather, cot, acc)
-
-    def keep_top(here):
-        top[here, :] = acc[here, :].astype(bf16)
-
-    row_pass(CLUSTER, keep_top)
-    for hop in range(3, zs):
-        d_gather.hop(hop)
-    d_gather.take_pair()
-    d_gather.finish()
+    act(PLAN[6])
 
     def down(t, span):
         acc[:, span] = mm(hidden[...], w_down[:, span])
@@ -792,15 +850,46 @@
     scatters = [
         GradScatter(links, w, f, b, place, zs, ctxs, p)
         for w, f, b, p in zip(
-            (w_qkv, w_out, w_up, g_down),
-            (sum_qkv, sum_out, sum_up, sum_down),
+            (
+                w_qkv,
+                w_out,
+                w_up,
+                g_down.at[:, pl.ds(0, back_split)],
+                g_down.at[:, pl.ds(back_split, width - back_split)],
+            ),
+            (
+                sum_qkv,
+                sum_out,
+                sum_up,
+                sum_down.at[:, pl.ds(0, back_split)],
+                sum_down.at[:, pl.ds(back_split, width - back_split)],
+            ),
             buffers,
             back_pairs,
         )
     ]
     gathered, links.sent = links.sent, []
     out_gather = CtxGather(links, result_low, all_out, ctx, wsh, ctxs, 2)
-    out_gather.advance()
+    back = {}
+
+    def go(plan):
+        for step in plan:
+            if step in back:
+                next(back[step], None)
+
+    def through(gather):
+        while gather.step < gather.steps:
+            gather.advance()
+            yield
+
+    def at_home(gather, own, target):
+        for _ in through(gather):
+            pass
+        bring_home(gather, own, target)
+        yield
+
+    back["l"] = through(out_gather)
+    go(BACK[0])
     part_rows = wide // (2 * zs)
 
     def down_grad(owner):
@@ -819,6 +908,7 @@
 
         down_grad(1 - core)
         scatters[3].send_core()
+        scatters[4].send_core()
         down_grad(core)
     else:
 
@@ -827,6 +917,7 @@
 
         tiles(wide, all_down)
         scatters[3].send_core()
+        scatters[4].send_core()
 
     def back_hidden(t, span):
         grad = (mm_nt(grad_low[...], w_down[span, :]) * slope[:, span]).astype(bf16)
@@ -836,9 +927,11 @@
         )
 
     tiles(wide // 2, back_hidden)
-    down_steps = scatters[3].steps()
-    next(down_steps)
+    back["d"] = scatters[3].steps()
+    back["e"] = scatters[4].steps()
+    go(BACK[1])
     tiles(wide, back_hidden, wide // 2)
+    go(BACK[2])
 
     def back_up(t, span):
         acc[:, span] = mm_nt(slope[...], w_up[span, :])
@@ -862,8 +955,7 @@
         tally(2, grad.astype(f32))
 
     row_pass(64, first_back)
-    while out_gather.step < out_gather.steps:
-        out_gather.advance()
+    go(BACK[3])
     for flight in gathered:
         flight.wait_send()
 
@@ -874,6 +966,7 @@
 
     tiles(wide, up_grad)
     scatters[2].send_core()
+    back["u"] = scatters[2].steps()
 
     turned[...] = context[...].T
 
@@ -887,10 +980,8 @@
 
     tiles(width, out_grad)
     scatters[1].send_core()
-    up_steps = scatters[2].steps()
-    next(up_steps)
-    out_steps = scatters[1].steps()
-    next(out_steps)
+    back["o"] = scatters[1].steps()
+    go(BACK[4])
 
     def back_attend(b, carry):
         here = pl.ds(pl.multiple_of(b * CLUSTER, CLUSTER), CLUSTER)
@@ -909,7 +1000,9 @@
                 qkv[here, at : at + LANES] = value.astype(bf16)
         return carry
 
-    lax.fori_loop(0, blocks, back_attend, 0)
+    for b in range(blocks):
+        lax.fori_loop(b, b + 1, back_attend, 0)
+        go(BACK[5 + min(b, 3)])
 
     def input_sums(here):
         tally(0, qkv[here, 0:width].astype(f32))
@@ -920,7 +1013,10 @@
     def back_qkv(t, span):
         back_low[:, span] = (mm_nt(qkv[...], w_qkv[span, :]) + grad_wide[:, span]).astype(bf16)
 
+    table = TableSum(links, small, small_slots, place, zs, ctxs)
+    back["s"] = table.steps()
     tiles(width, back_qkv)
+    go(BACK[9])
     grad_gather = CtxGather(links, back_low, all_grad, ctx, wsh, ctxs, 2)
     turned[...] = inputs[...].T
 
@@ -929,34 +1025,14 @@
 
     tiles(3 * width, qkv_grad)
     scatters[0].send_core()
-    table = TableSum(links, small, small_slots, place, zs, ctxs)
-    table_steps = table.steps()
-    next(table_steps)
-    next(out_steps)
-    bring_home(out_gather, result_low, home_out)
-    qkv_steps = scatters[0].steps()
-    next(qkv_steps)
-    grad_gather.advance()
-    next(table_steps)
-    next(up_steps)
-    while grad_gather.step < grad_gather.steps:
-        grad_gather.advance()
-    next(down_steps)
-    next(qkv_steps)
-    next(down_steps)
-    next(out_steps)
-    next(table_steps)
-    next(down_steps)
-    next(out_steps)
-    next(up_steps)
-    bring_home(grad_gather, back_low, home_grad)
-    running = [down_steps, out_steps, up_steps, table_steps, qkv_steps]
+    back["q"] = scatters[0].steps()
+    back["g"] = through(grad_gather)
+    back["H"] = at_home(out_gather, result_low, home_out)
+    back["K"] = at_home(grad_gather, back_low, home_grad)
+    go(BACK[10])
+    running = list(back.values())
     while running:
-        still = []
-        for steps in running:
-            if next(steps, "end") != "end":
-                still.append(steps)
-        running = still
+        running = [steps for steps in running if next(steps, "end") != "end"]
     count = width // STEP
     for n in range(8):
         for t in range(count):
@@ -1028,10 +1104,11 @@
     def vmem(shape, dtype=bf16):
         return pltpu.VMEM(shape, dtype)
 
-    pairs = (1, 1, 2, None)
-    back_pairs = (2, 2, 1, None)
+    pairs, back_pairs = PAIRS, BACK_PAIRS
     landing = []
-    for (n, columns), pair in zip(shards, back_pairs):
+    rows_down = down_weight.shape[0]
+    pieces = shards[:3] + [(rows_down, BACK_SPLIT), (rows_down, width - BACK_SPLIT)]
+    for (n, columns), pair in zip(pieces, back_pairs):
         part = columns // 2
         landing.append(vmem((zs, n, columns)))
         if pair is None:

time: 248 us -> 221 us (0.89)
  Pallas kernels: 247 us -> 219 us
    pallas_call x1, Pallas kernels: 241 us -> 214 us  [on_device(): pl.pallas_call(functools.partial(layer_kernel, ctxs, zs, pairs, back_pair...]
where the time goes in v4:
time: 221 us; the launch traced here: 220 us
  Pallas kernels  219 us (99%)
    pallas_call x1, Pallas kernels, on_device(): pl.pallas_call(functools.partial(layer_kernel, ctxs, zs, pairs, back_pair...  214 us
    pallas_call x1, Pallas kernels, on_device(): pl.pallas_call(functools.partial(finish_kernel, wshs), out_shape=outs, in...  5.39 us

profile of v4, /device:TPU:0, one launch (start us, length us, event | category | flops | bytes accessed | tf_op | source)
XLA Modules:
  0.0 219.8 jit_solution(4110054378996150316)
XLA Ops:
  0.7 213.5 %layer.1 = (bf16[512,768]{1,0:T(8,128)(2,1)}, bf16[512,768]{1,0:T(8,128)(2,1)}, bf16[96,2304]{1,0:T(8,128)(2,1)}, bf16[96,768]{1,0:T(8,128)(2,1)}, bf16[96,3072]...) custom-call(bf16[512,768]{1,0:T(8,128)(2,1)} %bitcast.4, ...), custom_call_target="tpu_custom_call" | custom-call | tf_op jit(solution)/shard_map/layer/pallas_call | solution.py:1127
  214.2 5.4 %finish.1 = (bf16[512,768]{1,0:T(8,128)(2,1)}, f32[512,768]{1,0:T(8,128)}, f32[96,2304]{1,0:T(8,128)}, f32[96,768]{1,0:T(8,128)}, f32[96,3072]{1,0:T(8,128)}, /*...) custom-call(bf16[512,768]{1,0:T(8,128)(2,1)} %get-tuple-element.38.r, ...), custom_call_target="tpu_custom_call" | custom-call | tf_op jit(solution)/shard_map/finish/pallas_call | solution.py:1203

commit v5 on v4

--- a/solution.py
+++ b/solution.py
@@ -145,6 +145,89 @@
             if have[offset] is not None:
                 have[offset].wait_recv()
                 have[offset] = None
+
+
+class RowRoute:
+    def __init__(self, links, buffer, place, count, cap, shared):
+        self.links, self.buffer = links, buffer
+        self.ctx, self.wsh = place
+        self.count, self.cap = count, cap
+        self.rows_out, self.landed, self.using = shared
+        self.kept, self.flights, self.passing = {}, {}, {}
+
+    def block(self, of):
+        return pl.ds(pl.multiple_of(of * self.cap, 16), self.cap)
+
+    def free(self, phase):
+        for flight in self.using.pop(phase, []):
+            flight.wait_send()
+
+    def send(self, phase):
+        flights = {}
+        leaving = []
+        slot = phase * self.count
+        for offset in sorted(range(1, self.count), reverse=self.count == 4):
+            to = flip(self.ctx, offset)
+            rows = self.rows_out.at[phase, self.block(to)]
+            if self.count == 4 and offset == 3:
+                passing = self.links.send(
+                    rows, self.buffer.at[2 * self.count + phase], flip(self.ctx, 1), self.wsh
+                )
+                self.passing[phase] = passing
+                leaving.append(passing)
+                continue
+            flights[offset] = self.links.send(
+                rows,
+                self.buffer.at[slot + self.ctx],
+                to,
+                self.wsh,
+                landing=self.buffer.at[slot + to],
+            )
+        self.flights[phase] = flights
+        kept = Kept(
+            self.links.local(
+                self.rows_out.at[phase, self.block(self.ctx)], self.buffer.at[slot + self.ctx]
+            )
+        )
+        self.kept[phase] = kept
+        self.using[phase] = leaving + list(flights.values()) + [kept]
+
+    def forward(self, phase):
+        if self.count == 4:
+            self.passing[phase].wait_recv()
+            slot = phase * self.count
+            self.flights[phase][3] = self.links.send(
+                self.buffer.at[2 * self.count + phase],
+                self.buffer.at[slot + flip(self.ctx, 1)],
+                flip(self.ctx, 2),
+                self.wsh,
+                landing=self.buffer.at[slot + flip(self.ctx, 3)],
+            )
+
+    def collect(self, phase):
+        self.kept[phase].wait_send()
+        copies = []
+        for offset in range(self.count):
+            if offset > 0:
+                self.flights[phase][offset].wait_recv()
+            of = flip(self.ctx, offset)
+            copies.append(
+                self.links.local(
+                    self.buffer.at[phase * self.count + of], self.landed.at[self.block(of)]
+                )
+            )
+        for copy in copies:
+            copy.wait()
+
+
+class Kept:
+    def __init__(self, copy):
+        self.copy, self.leaving = copy, True
+
+    def wait_send(self):
+        if self.leaving:
+            self.copy.wait()
+        self.leaving = False
 
 
 class WeightGather:
@@ -426,34 +509,34 @@
         yield
 
 
-DOWN_SPLIT = 256
-BACK_SPLIT = 512
-PAIRS = (1, 2, 2, 1)
+DOWN_SPLIT = 512
+BACK_SPLIT = 256
+PAIRS = (2, 1, 1, 2)
 BACK_PAIRS = (1, 2, 2, None, 1)
 PLAN = (
-    ("t", "q0", "o0", "u0", "tx", "q1", "u1", "q2", "o1", "o2", "q3",),
-    ("u2", "e0", "d0", "r", "o3",),
-    ("u3", "c", "qp", "e1", "op", "qf",),
-    ("of",),
-    ("e2", "d1", "e3", "cx",),
-    ("up", "ep", "d2", "uf",),
-    ("d3", "P", "df", "rx", "ef",),
+    ("o0", "q0", "u0", "t", "e0", "i1", "o1", "i2", "i3", "tx", "c", "q1", "u1", "o2",),
+    ("q2", "cr", "o3", "u2", "q3", "e1",),
+    ("d0", "u3", "e2", "qp", "cx", "qf", "op",),
+    ("d1", "i4",),
+    ("of", "up", "e3",),
+    ("uf", "d2", "cy",),
+    ("ep", "d3", "P", "ef", "df",),
 )
 BACK = (
     ("l",),
     (),
-    ("d", "e", "l",),
+    ("l", "d", "e",),
+    ("l", "d",),
+    ("e",),
+    (),
+    ("u", "d", "e",),
     (),
     (),
-    ("e", "d",),
-    (),
-    ("u",),
-    ("e",),
-    (),
+    ("s", "d", "u", "e",),
     (
-        "e", "s", "u", "q", "q", "e", "d", "e", "o", "u", "e", "H", "g", "o", "o", "s", "u",
-        "d", "q", "u", "q", "o", "u", "e", "u", "q", "g", "q", "e", "u", "o", "o", "o", "q",
-        "s", "d", "q", "o", "s", "u", "q", "K", "o", "u", "e", "d", "s", "q", "o",
+        "o", "s", "u", "q", "q", "e", "u", "e", "g", "d", "q", "u", "u", "s", "q", "o", "g",
+        "e", "o", "l", "g", "o", "q", "q", "s", "g", "e", "q", "o", "o", "u", "s", "u", "g",
+        "d", "o", "q", "u", "e", "o", "q", "o", "l", "q", "o", "e", "u",
     ),
 )
 
@@ -495,13 +578,18 @@
     order_column,
     vectors,
     all_order,
+    places,
+    route_home,
+    route_middle,
+    route_cluster,
+    rows_out,
+    landed,
     all_vectors,
     w_qkv,
     w_out,
     w_up,
     w_down,
     g_down,
-    stage,
     acc,
     inputs,
     low,
@@ -560,14 +648,20 @@
         for same in (True, False)
         if o > 0 or not same
     ]
-    peers = stream_peers + [(flip(ctx, b), wsh) for b in bits_of(ctxs)]
+    ctx_peers = [(flip(ctx, o), wsh) for o in range(1, ctxs)]
+    peers = stream_peers + ctx_peers
     for peer in peers:
         pl.semaphore_signal(barrier, 1, device_id=peer, device_id_type=pl.DeviceIdType.MESH)
     pl.semaphore_wait(barrier, len(peers))
 
     tok_gather = CtxGather(links, tok, all_tok, ctx, wsh, ctxs, 2)
-    cot_gather = CtxGather(links, cot, all_cot, ctx, wsh, ctxs, 2)
-    order_gather = CtxGather(links, order_block, all_order, ctx, wsh, ctxs, 1)
+    cap = route_home.shape[0] // ctxs
+    shared = (rows_out, landed, {})
+    cot_route, out_route, grad_route = [
+        RowRoute(links, buffer, (ctx, wsh), ctxs, cap, shared)
+        for buffer in (all_cot, all_out, all_grad)
+    ]
+    order_flights = [links.send(order_block, all_order.at[ctx], *peer) for peer in ctx_peers]
     vec_own = links.local(vectors, all_vectors.at[wsh])
     vec_flights = [links.send(vectors, all_vectors.at[wsh], *peer) for peer in stream_peers]
     split = DOWN_SPLIT
@@ -585,13 +679,12 @@
     weights = dict(
         zip("quoed", [WeightGather(links, *parts[n], place, zs) for n in (0, 2, 1, 3, 4)])
     )
-    rows_in = {"t": tok_gather, "r": order_gather, "c": cot_gather}
+    rows_in = {"t": tok_gather}
 
     def act(plan):
         for step in plan:
-            if step == "P":
-                pick(cot_gather, cot, acc)
-                row_pass(CLUSTER, keep_top)
+            if step in routing:
+                routing[step]()
                 continue
             if step[0] in rows_in:
                 gather = rows_in[step[0]]
@@ -613,6 +706,156 @@
             else:
                 gather.finish()
 
+    def tiles(columns, body, first=0):
+        def step(t, carry):
+            body(t, pl.ds(pl.multiple_of(t * STEP, STEP), STEP))
+            return carry
+
+        lax.fori_loop(first // STEP, columns // STEP, step, 0)
+
+    def token_at(s):
+        return lax.broadcasted_iota(jnp.int32, (rows, rows), 0) + s * rows
+
+    def ones_where(condition):
+        return jnp.where(condition, 1.0, 0.0).astype(bf16)
+
+    def destinations():
+        for flight in order_flights:
+            flight.wait_recv()
+        all_order[ctx] = order[...]
+        places[...] = jnp.zeros_like(places)
+
+        def class_body(d, carry):
+            column = jnp.broadcast_to(all_order[d].astype(f32), (LANES, rows)).T
+            lane = lax.broadcasted_iota(jnp.int32, (rows, LANES), 1).astype(f32)
+            for t in range(ctxs * rows // LANES):
+                here = slice(t * LANES, (t + 1) * LANES)
+                taken = jnp.where(column == lane + t * LANES, 1.0, 0.0)
+                found = jnp.sum(taken, axis=0, keepdims=True)
+                places[3:4, here] = places[3:4, here] + found * d.astype(f32)
+            return carry
+
+        lax.fori_loop(1, ctxs, class_body, 0)
+
+    def slots():
+        def slot_body(once, carry):
+            before = route_cluster.at[0:rows]
+            before[...] = ones_where(
+                lax.broadcasted_iota(jnp.int32, (rows, rows), 0)
+                < lax.broadcasted_iota(jnp.int32, (rows, rows), 1)
+            )
+            row8 = lax.broadcasted_iota(jnp.int32, (8, rows), 0).astype(f32)
+            pairs_row = lax.broadcasted_iota(jnp.int32, (ctxs * ctxs, rows), 0).astype(f32)
+            gone = jnp.zeros((ctxs * ctxs, 1), f32)
+            for s in range(ctxs):
+                here = slice(s * rows, (s + 1) * rows)
+
+                def rank(marks):
+                    return mm(marks.astype(bf16), before[...])
+
+                to = places[3:4, here]
+                mark = jnp.where(row8 == to, 1.0, 0.0)
+                turn = jnp.sum(mark * rank(mark), axis=0, keepdims=True) + to + s
+                middle = turn - ctxs * jnp.floor(turn * (1.0 / ctxs))
+                mark = jnp.where(row8 == middle, 1.0, 0.0)
+                places[0:1, here] = middle
+                places[1:2, here] = jnp.sum(mark * rank(mark), axis=0, keepdims=True)
+                mark = jnp.where(pairs_row == middle * ctxs + to, 1.0, 0.0)
+                places[2:3, here] = jnp.sum(mark * (rank(mark) + gone), axis=0, keepdims=True)
+                gone = gone + jnp.sum(mark, axis=1, keepdims=True)
+            mine = pl.ds(pl.multiple_of(ctx * rows, LANES), rows)
+            code = (places[0:1, mine] * cap + places[1:2, mine]).astype(jnp.int32)
+            route_home[...] = ones_where(slot_row(ctxs) == code)
+            return carry
+
+        lax.fori_loop(0, 1, slot_body, 0)
+
+    def slot_row(blocks_of):
+        return lax.broadcasted_iota(jnp.int32, (blocks_of * cap, rows), 0)
+
+    def middle_route():
+        def middle_body(s, carry):
+            here = pl.ds(pl.multiple_of(s * rows, LANES), rows)
+            middle, first, second, to = [
+                places[n : n + 1, here].astype(jnp.int32) for n in range(4)
+            ]
+            coming = ones_where((slot_row(1) == first) & (middle == ctx))
+            going = ones_where(slot_row(ctxs) == to * cap + second)
+            at = pl.ds(pl.multiple_of(s * cap, 16), cap)
+            route_middle[at, :] = mm_nt(coming, going).astype(bf16)
+            return carry
+
+        lax.fori_loop(0, ctxs, middle_body, 0)
+
+    def cluster_route():
+        route_cluster[...] = jnp.zeros_like(route_cluster)
+
+        def cluster_body(s, carry):
+            here = pl.ds(pl.multiple_of(s * rows, LANES), rows)
+            code = (places[0:1, here] * cap + places[2:3, here]).astype(jnp.int32)
+            sits = ones_where(slot_row(ctxs) == code)
+            taken = ones_where(order[...] == token_at(s))
+            route_cluster[...] = (route_cluster[...].astype(f32) + mm(sits, taken)).astype(bf16)
+            return carry
+
+        lax.fori_loop(0, ctxs, cluster_body, 0)
+
+    def hop(route, phase, product, matrix, source):
+        route.free(phase)
+
+        def sort_rows(t, span):
+            rows_out[phase, :, span] = product(matrix[...], source[:, span]).astype(bf16)
+
+        tiles(width, sort_rows)
+        route.send(phase)
+
+    def arrive(route, product, matrix, target):
+        route.collect(1)
+
+        def place_rows(t, span):
+            target[:, span] = product(matrix[...], landed[:, span]).astype(bf16)
+
+        tiles(width, place_rows)
+
+    def cot_first():
+        links.local(cot, landed.at[0:rows]).wait()
+        hop(cot_route, 0, mm, route_home, landed.at[0:rows])
+
+    def cot_second():
+        cot_route.collect(0)
+        hop(cot_route, 1, mm_tn, route_middle, landed)
+
+    def cot_last():
+        arrive(cot_route, mm_tn, route_cluster, top)
+
+    routing = {
+        "i1": destinations,
+        "i2": slots,
+        "i3": middle_route,
+        "i4": cluster_route,
+        "c": cot_first,
+        "cr": functools.partial(cot_route.forward, 0),
+        "cx": cot_second,
+        "cy": functools.partial(cot_route.forward, 1),
+        "P": cot_last,
+    }
+
+    leaving = []
+
+    def go_home(route, source, buffer, target):
+        hop(route, 0, mm, route_cluster, source)
+        yield
+        route.forward(0)
+        yield
+        route.collect(0)
+        hop(route, 1, mm, route_middle, landed)
+        yield
+        route.forward(1)
+        yield
+        arrive(route, mm_tn, route_home, buffer)
+        leaving.append(links.local(buffer, target))
+        yield
+
     act(PLAN[0])
     vec_own.wait()
     for flight in vec_flights:
@@ -640,11 +883,9 @@
         else:
             spread(all_vectors[s, 8:16, :], length_up * s, length_up, row_up)
 
-    def keep_top(here):
-        top[here, :] = acc[here, :].astype(bf16)
-
     def pick(gather, own, total):
         copies = {}
+        stage = (result_low, back_low)
 
         def fetch(offset):
             if offset == 0:
@@ -652,7 +893,7 @@
             else:
                 gather.need(offset)
                 src = gather.buffer.at[flip(ctx, offset)]
-            copies[offset] = links.local(src, stage.at[offset % 2])
+            copies[offset] = links.local(src, stage[offset % 2])
 
         fetch(0)
         for offset in range(ctxs):
@@ -672,57 +913,11 @@
                     ],
                     axis=1,
                 )
-                got = mm(chosen, stage[offset % 2])
+                got = mm(chosen, stage[offset % 2][...])
                 total[here, :] = got if offset == 0 else total[here, :] + got
                 return carry
 
             lax.fori_loop(0, blocks, body, 0)
-
-    def bring_home(gather, own, target):
-        copies = {}
-
-        def fetch(offset):
-            if offset == 0:
-                src = own
-            else:
-                gather.need(offset)
-                src = gather.buffer.at[flip(ctx, offset)]
-            copies[offset] = links.local(src, stage.at[offset % 2])
-
-        fetch(0)
-        for offset in range(ctxs):
-            copies[offset].wait()
-            if offset + 1 < ctxs:
-                fetch(offset + 1)
-            if offset == 0:
-                places = order[...]
-            else:
-                order_gather.need(offset)
-                places = all_order[flip(ctx, offset)]
-
-            def body(i, carry):
-                here = pl.ds(pl.multiple_of(i * CLUSTER, CLUSTER), CLUSTER)
-                token = lax.broadcasted_iota(jnp.int32, (CLUSTER, rows), 0) + (
-                    ctx * rows + i * CLUSTER
-                )
-                chosen = jnp.where(places[0:1, :] == token, 1.0, 0.0).astype(bf16)
-                got = mm(chosen, stage[offset % 2])
-                if offset > 0:
-                    got = acc[here, :] + got
-                if offset == ctxs - 1:
-                    target[here, :] = got.astype(bf16)
-                else:
-                    acc[here, :] = got
-                return carry
-
-            lax.fori_loop(0, blocks, body, 0)
-
-    def tiles(columns, body, first=0):
-        def step(t, carry):
-            body(t, pl.ds(pl.multiple_of(t * STEP, STEP), STEP))
-            return carry
-
-        lax.fori_loop(first // STEP, columns // STEP, step, 0)
 
     def row_pass(size, body):
         def step(i, carry):
@@ -869,7 +1064,6 @@
         )
     ]
     gathered, links.sent = links.sent, []
-    out_gather = CtxGather(links, result_low, all_out, ctx, wsh, ctxs, 2)
     back = {}
 
     def go(plan):
@@ -877,18 +1071,7 @@
             if step in back:
                 next(back[step], None)
 
-    def through(gather):
-        while gather.step < gather.steps:
-            gather.advance()
-            yield
-
-    def at_home(gather, own, target):
-        for _ in through(gather):
-            pass
-        bring_home(gather, own, target)
-        yield
-
-    back["l"] = through(out_gather)
+    back["l"] = go_home(out_route, result_low, low, home_out)
     go(BACK[0])
     part_rows = wide // (2 * zs)
 
@@ -1017,7 +1200,6 @@
     back["s"] = table.steps()
     tiles(width, back_qkv)
     go(BACK[9])
-    grad_gather = CtxGather(links, back_low, all_grad, ctx, wsh, ctxs, 2)
     turned[...] = inputs[...].T
 
     def qkv_grad(t, span):
@@ -1026,9 +1208,7 @@
     tiles(3 * width, qkv_grad)
     scatters[0].send_core()
     back["q"] = scatters[0].steps()
-    back["g"] = through(grad_gather)
-    back["H"] = at_home(out_gather, result_low, home_out)
-    back["K"] = at_home(grad_gather, back_low, home_grad)
+    back["g"] = go_home(grad_route, back_low, top, home_grad)
     go(BACK[10])
     running = list(back.values())
     while running:
@@ -1040,6 +1220,8 @@
     for t in range(wide // STEP):
         sum_wide[0:1, t * STEP : (t + 1) * STEP] = small[8 * count + t : 8 * count + t + 1]
     links.drain()
+    for copy in leaving:
+        copy.wait()
     for scatter in scatters:
         for result in scatter.results:
             result.wait()
@@ -1124,6 +1306,8 @@
     anywhere = pl.BlockSpec(memory_space=pl.ANY)
     on_chip = pl.BlockSpec(memory_space=pltpu.VMEM)
     many = jax.ShapeDtypeStruct((ctxs, rows, width), bf16)
+    cap = (rows // ctxs + ctxs - 1 + 15) // 16 * 16
+    routed = jax.ShapeDtypeStruct((2 * ctxs + 2, cap, width), bf16)
     results = pl.pallas_call(
         functools.partial(layer_kernel, ctxs, zs, pairs, back_pairs),
         out_shape=[
@@ -1132,20 +1316,25 @@
         ]
         + [jax.ShapeDtypeStruct(s, bf16) for s in shards]
         + [jax.ShapeDtypeStruct((8, width), f32), jax.ShapeDtypeStruct((8, wide), f32)]
-        + [many] * 4,
+        + [many] + [routed] * 3,
         in_specs=[anywhere, anywhere, on_chip, anywhere] + [anywhere] * 13,
-        out_specs=[on_chip, on_chip] + [anywhere] * 4 + [on_chip] * 2 + [anywhere] * 4,
+        out_specs=[anywhere] * 6 + [on_chip] * 2 + [anywhere] * 4,
         scratch_shapes=[
             vmem((rows, LANES), jnp.int32),
             vmem((16, vector_lanes)),
             vmem((ctxs, 1, rows), jnp.int32),
+            vmem((8, ctxs * rows), f32),
+            vmem((ctxs * cap, rows)),
+            vmem((ctxs * cap, ctxs * cap)),
+            vmem((ctxs * cap, rows)),
+            vmem((2, ctxs * cap, width)),
+            vmem((ctxs * cap, width)),
             vmem((wshs, 16, vector_lanes)),
             vmem((width, 3 * width)),
             vmem((width, width)),
             vmem((width, wide)),
             vmem((wide, width)),
             vmem((wide, width)),
-            vmem((2, rows, width)),
             vmem((rows, width), f32),
             vmem((rows, width)),
             vmem((rows, width)),

time: 221 us -> 214 us (0.968)
  Pallas kernels: 219 us -> 212 us
    pallas_call x1, Pallas kernels: 214 us -> 207 us  [on_device(): pl.pallas_call(functools.partial(layer_kernel, ctxs, zs, pairs, back_pair...]
where the time goes in v5:
time: 214 us; the launch traced here: 213 us
  Pallas kernels  212 us (99%)
    pallas_call x1, Pallas kernels, on_device(): pl.pallas_call(functools.partial(layer_kernel, ctxs, zs, pairs, back_pair...  207 us
    pallas_call x1, Pallas kernels, on_device(): pl.pallas_call(functools.partial(finish_kernel, wshs), out_shape=outs, in...  5.39 us

profile of v5, /device:TPU:0, one launch (start us, length us, event | category | flops | bytes accessed | tf_op | source)
XLA Modules:
  0.0 213.3 jit_solution(13265665080875379421)
XLA Ops:
  0.7 207.1 %layer.1 = (bf16[512,768]{1,0:T(8,128)(2,1)}, bf16[512,768]{1,0:T(8,128)(2,1)}, bf16[96,2304]{1,0:T(8,128)(2,1)}, bf16[96,768]{1,0:T(8,128)(2,1)}, bf16[96,3072]...) custom-call(bf16[512,768]{1,0:T(8,128)(2,1)} %bitcast.4, ...), custom_call_target="tpu_custom_call" | custom-call | tf_op jit(solution)/shard_map/layer/pallas_call | solution.py:1311
  207.7 5.4 %finish.1 = (bf16[512,768]{1,0:T(8,128)(2,1)}, f32[512,768]{1,0:T(8,128)}, f32[96,2304]{1,0:T(8,128)}, f32[96,768]{1,0:T(8,128)}, f32[96,3072]{1,0:T(8,128)}, /*...) custom-call(bf16[512,768]{1,0:T(8,128)(2,1)} %get-tuple-element.38.r, ...), custom_call_target="tpu_custom_call" | custom-call | tf_op jit(solution)/shard_map/finish/pallas_call | solution.py:1392
